TPU v7x, 128 devices: a whole 4x4x4 slice. The times are simulated.
128 devices in a mesh: section: 8 (over x_hi, y), dp: 16 (over z, x_lo, core).
Axes of the slice: x: 4 (x_hi: 2, x_lo: 2; x = x_hi * 2 + x_lo), y: 4, z: 4, core: 2. Of those that a mesh axis runs over, the one named last changes fastest.
Arguments:
- section_inputs: bfloat16 [2, 8, 4, 2048, 1024], P(None, 'section', None, 'dp'), may hold values from -6 to 6
- top_grad: bfloat16 [2, 4, 2048, 1024], P(None, None, 'dp'), may hold values from -0.125 to 0.125
- plan: int32 [2, 4], replicated, may hold values from 0 to 3, each once within a row
- up_weight: bfloat16 [2, 8, 1024, 2048], P(None, 'section'), as said below
- down_weight: bfloat16 [2, 8, 2048, 1024], P(None, 'section'), as said below
- up_moment: float32 [8, 1024, 2048], P('section', 'dp'), may hold values from -6 to 6
- down_moment: float32 [8, 2048, 1024], P('section', 'dp'), may hold values from -6 to 6
Outputs:
- new_up_weight: bfloat16 [2, 8, 1024, 2048], P(None, 'section', 'dp')
- new_down_weight: bfloat16 [2, 8, 2048, 1024], P(None, 'section', 'dp')
- new_up_moment: float32 [8, 1024, 2048], P('section', 'dp')
- new_down_moment: float32 [8, 2048, 1024], P('section', 'dp')
Inputs may be any that keep to these rules, and one draw needn't show every extreme that they name: up_weight[1, s] equals up_weight[0, 7 - s] for every s: both relays hold the same model. down_weight[1, s] equals down_weight[0, 7 - s] for every s. `plan`: each row names every micro-batch once.
All inputs are finite; a program needn't handle non-finite values.
Results may differ from a plain program's by a relative error of at most 0.02.
Values may be sent and summed in bfloat16 or wider, within the bound.
A program may use at most 128 MiB of HBM per device.

v0:
```python
import jax
import jax.numpy as jnp
from jax import lax
from jax.sharding import PartitionSpec as P

norm_epsilon = 1e-06
momentum_decay = 0.9
step_size = 0.01
root_half = 0.7071067811865476
inv_root_tau = 0.3989422804014327


def for_sending(x):

    def short(part):
        return part.astype(jnp.bfloat16) if part.dtype == jnp.float32 else part

    return jax.tree.map(short, x)


def from_behind(value, axis, steps):
    count = lax.axis_size(axis)
    leading, last = (max(0, -steps), min(count, count - steps))
    return lax.ppermute(value, axis, [(source, source + steps) for source in range(leading, last)])


def partner(x, axis, bit):
    return lax.ppermute(x, axis, [(i, i ^ 1 << bit) for i in range(lax.axis_size(axis))])


def gelu_value(preact):
    return 0.5 * preact * (1.0 + lax.erf(preact * root_half))


def gelu_slope(preact):
    return (
        0.5 * (1.0 + lax.erf(preact * root_half))
        + preact * jnp.exp(-0.5 * preact * preact) * inv_root_tau
    )


def times_transpose(left, right):
    return lax.dot_general(
        left, right, (((1,), (1,)), ((), ())), preferred_element_type=jnp.float32
    )


def contract_rows(left, right):
    return lax.dot_general(
        left, right, (((0,), (0,)), ((), ())), preferred_element_type=jnp.float32
    )


def local_backward(inputs, incoming, w_up, w_down):
    preact = jnp.dot(inputs, w_up, preferred_element_type=jnp.float32)
    hidden = gelu_value(preact).astype(jnp.bfloat16)
    summed = inputs.astype(jnp.float32) + jnp.dot(
        hidden, w_down, preferred_element_type=jnp.float32
    )
    centre = summed - jnp.mean(summed, axis=-1, keepdims=True)
    scale_inv = lax.rsqrt(jnp.mean(centre * centre, axis=-1, keepdims=True) + norm_epsilon)
    normed = centre * scale_inv
    upstream = incoming.astype(jnp.float32)
    grad_sum = scale_inv * (
        upstream
        - jnp.mean(upstream, axis=-1, keepdims=True)
        - normed * jnp.mean(upstream * normed, axis=-1, keepdims=True)
    )
    grad_sum_low = grad_sum.astype(jnp.bfloat16)
    grad_pre = (times_transpose(grad_sum_low, w_down) * gelu_slope(preact)).astype(jnp.bfloat16)
    grad_in = (grad_sum + times_transpose(grad_pre, w_up)).astype(jnp.bfloat16)
    return (grad_in, hidden, grad_pre, grad_sum_low)


def on_device(section_inputs, top_grad, plan, up_weight, down_weight, up_moment, down_moment):
    sections = lax.axis_size("section")
    position = lax.axis_index("section")
    micro = top_grad.shape[1]
    tokens = top_grad.shape[2]
    model = up_weight.shape[2]
    width = up_weight.shape[3]
    ordered = [section_inputs[direction, 0][plan[direction]] for direction in range(2)]
    starts = (sections - 1 - position, position)
    entries = (position == sections - 1, position == 0)

    def keep(state, slot, hidden, grad_pre, grad_sum_low):
        return (
            lax.dynamic_update_index_in_dim(state[0], hidden, slot, 0),
            lax.dynamic_update_index_in_dim(state[1], grad_pre, slot, 0),
            lax.dynamic_update_index_in_dim(state[2], grad_sum_low, slot, 0),
        )

    blank = (
        jnp.zeros((micro, tokens, width), jnp.bfloat16),
        jnp.zeros((micro, tokens, width), jnp.bfloat16),
        jnp.zeros((micro, tokens, model), jnp.bfloat16),
    )
    states = (blank, blank)

    def work(operand):
        state, incoming, inputs, slot, w_up, w_down = operand
        grad_in, hidden, grad_pre, grad_sum_low = local_backward(inputs, incoming, w_up, w_down)
        return (grad_in, keep(state, slot, hidden, grad_pre, grad_sum_low))

    def skip(operand):
        return (jnp.zeros_like(operand[1]), operand[0])

    def advance(tick, received, states):
        sent = []
        kept = []
        for direction in range(2):
            slot = tick - starts[direction]
            active = jnp.logical_and(slot >= 0, slot < micro)
            slot_safe = jnp.clip(slot, 0, micro - 1)
            inputs = lax.dynamic_index_in_dim(ordered[direction], slot_safe, 0, keepdims=False)
            arrived = lax.dynamic_index_in_dim(top_grad[direction], slot_safe, 0, keepdims=False)
            incoming = jnp.where(entries[direction], arrived, received[direction])
            operand = (
                states[direction],
                incoming,
                inputs,
                slot_safe,
                up_weight[direction, 0],
                down_weight[direction, 0],
            )
            grad_in, state = lax.cond(active, work, skip, operand)
            sent.append(grad_in)
            kept.append(state)
        return ((sent[0], sent[1]), (kept[0], kept[1]))

    def loop_step(tick, carry):
        received, states = carry
        sent, states = advance(tick, received, states)
        down_next = from_behind(for_sending(sent[0]), "section", -1)
        up_next = from_behind(for_sending(sent[1]), "section", 1)
        return ((down_next, up_next), states)

    empty = jnp.zeros((tokens, model), jnp.bfloat16)
    received, states = lax.fori_loop(0, sections + micro - 2, loop_step, ((empty, empty), states))
    sent, states = advance(sections + micro - 2, received, states)
    rows_up = up_moment.shape[1]
    rows_down = down_moment.shape[1]
    flat_inputs = [ordered[direction].reshape(micro * tokens, model) for direction in range(2)]
    flat_hidden = [states[direction][0].reshape(micro * tokens, width) for direction in range(2)]
    flat_pre = [states[direction][1].reshape(micro * tokens, width) for direction in range(2)]
    flat_sum = [states[direction][2].reshape(micro * tokens, model) for direction in range(2)]
    parts = [contract_rows(flat_inputs[direction], flat_pre[direction]) for direction in range(2)]
    summed_up = lax.psum_scatter(
        jnp.concatenate(parts, axis=1).astype(jnp.bfloat16), "dp", scatter_dimension=0, tiled=True
    ).astype(jnp.float32)
    parts = [contract_rows(flat_hidden[direction], flat_sum[direction]) for direction in range(2)]
    summed_down = lax.psum_scatter(
        jnp.concatenate(parts, axis=1).astype(jnp.bfloat16), "dp", scatter_dimension=0, tiled=True
    ).astype(jnp.float32)
    own_up, far_up = (summed_up[:, :width], summed_up[:, width:])
    own_down, far_down = (summed_down[:, :model], summed_down[:, model:])
    replica = lax.axis_index("dp")
    up_rows_held = lax.dynamic_slice_in_dim(up_weight[:, 0], replica * rows_up, rows_up, 1)
    down_rows_held = lax.dynamic_slice_in_dim(down_weight[:, 0], replica * rows_down, rows_down, 1)
    bits = sections.bit_length() - 1
    parcel = (own_up, own_down, far_up, far_down, up_moment[0], down_moment[0])
    for bit in range(bits):
        parcel = (
            partner(parcel[0].astype(jnp.bfloat16), "section", bit).astype(jnp.float32),
            partner(parcel[1].astype(jnp.bfloat16), "section", bit).astype(jnp.float32),
            partner(parcel[2].astype(jnp.bfloat16), "section", bit).astype(jnp.float32),
            partner(parcel[3].astype(jnp.bfloat16), "section", bit).astype(jnp.float32),
            partner(parcel[4].astype(jnp.bfloat16), "section", bit).astype(jnp.float32),
            partner(parcel[5].astype(jnp.bfloat16), "section", bit).astype(jnp.float32),
        )
    (
        their_own_up,
        their_own_down,
        their_far_up,
        their_far_down,
        their_moment_up,
        their_moment_down,
    ) = parcel
    moment_up_new = momentum_decay * up_moment[0] + (own_up + their_far_up)
    moment_down_new = momentum_decay * down_moment[0] + (own_down + their_far_down)
    fresh_up = (up_rows_held[0].astype(jnp.float32) - step_size * moment_up_new).astype(
        jnp.bfloat16
    )
    fresh_down = (down_rows_held[0].astype(jnp.float32) - step_size * moment_down_new).astype(
        jnp.bfloat16
    )
    mirror_moment_up = momentum_decay * their_moment_up + (their_own_up + far_up)
    mirror_moment_down = momentum_decay * their_moment_down + (their_own_down + far_down)
    mirror_fresh_up = (up_rows_held[1].astype(jnp.float32) - step_size * mirror_moment_up).astype(
        jnp.bfloat16
    )
    mirror_fresh_down = (
        down_rows_held[1].astype(jnp.float32) - step_size * mirror_moment_down
    ).astype(jnp.bfloat16)
    new_up_weight = jnp.stack([fresh_up, mirror_fresh_up])[:, None]
    new_down_weight = jnp.stack([fresh_down, mirror_fresh_down])[:, None]
    return (new_up_weight, new_down_weight, moment_up_new[None], moment_down_new[None])


def solution(mesh):
    in_specs = (
        P(None, "section", None, "dp", None),
        P(None, None, "dp", None),
        P(),
        P(None, "section", None, None),
        P(None, "section", None, None),
        P("section", "dp", None),
        P("section", "dp", None),
    )
    out_specs = (
        P(None, "section", "dp", None),
        P(None, "section", "dp", None),
        P("section", "dp", None),
        P("section", "dp", None),
    )
    return jax.shard_map(
        on_device, mesh=mesh, in_specs=in_specs, out_specs=out_specs, check_vma=False
    )
```

profile of v0, /device:TPU:31, one launch (start us, length us, event | category | flops | bytes accessed | tf_op | source)
XLA Modules:
  0.0 628.5 jit_solution(6539688442643413216)
XLA Ops:
  21.8 268.6 %while.27 = (s32[]{:T(128)}, bf16[128,1024]{1,0:T(8,128)(2,1)S(1)}, bf16[128,1024]{1,0:T(8,128)(2,1)S(1)}, bf16[4,128,2048]{2,1,0:T(8,128)(2,1)}, bf16[4,128,204...) while((s32[]{:T(128)}, bf16[128,1024]{1,0:T(8,128)(2,1)S(1)}, ...), condition=%wide.region_13.14_spmd, body=%wide.region_0.13_spmd.sunk | while | flops 4315414528 | bytes 162559888 | solution.py:139
  23.2 12.9 %conditional.8 = (bf16[128,1024]{1,0:T(8,128)(2,1)S(1)}, bf16[4,128,2048]{2,1,0:T(8,128)(2,1)}, bf16[4,128,2048]{2,1,0:T(8,128)(2,1)}, bf16[4,128,1024]{2,1,0:T(8,128)(2,1)}) conditional(s32[]{:T(128)} %convert_element_type.440, (bf16[4,128,2048]{2,1,0:T(8,128)(2,1)}, bf16[4,128,2048]{2,1,0:T(8,128)(2,1)}, ...), branch_computations={%region_1.1_spmd, %region_2.6_spmd} | conditional | flops 2157707264 | bytes 80231088 | solution.py:126
  37.4 5.2 collective-permute-done
  44.0 12.9 %conditional.8 = (bf16[128,1024]{1,0:T(8,128)(2,1)S(1)}, bf16[4,128,2048]{2,1,0:T(8,128)(2,1)}, bf16[4,128,2048]{2,1,0:T(8,128)(2,1)}, bf16[4,128,1024]{2,1,0:T(8,128)(2,1)}) conditional(s32[]{:T(128)} %convert_element_type.440, (bf16[4,128,2048]{2,1,0:T(8,128)(2,1)}, bf16[4,128,2048]{2,1,0:T(8,128)(2,1)}, ...), branch_computations={%region_1.1_spmd, %region_2.6_spmd} | conditional | flops 2157707264 | bytes 80231088 | solution.py:126
  67.4 12.9 %conditional.8 = (bf16[128,1024]{1,0:T(8,128)(2,1)S(1)}, bf16[4,128,2048]{2,1,0:T(8,128)(2,1)}, bf16[4,128,2048]{2,1,0:T(8,128)(2,1)}, bf16[4,128,1024]{2,1,0:T(8,128)(2,1)}) conditional(s32[]{:T(128)} %convert_element_type.440, (bf16[4,128,2048]{2,1,0:T(8,128)(2,1)}, bf16[4,128,2048]{2,1,0:T(8,128)(2,1)}, ...), branch_computations={%region_1.1_spmd, %region_2.6_spmd} | conditional | flops 2157707264 | bytes 80231088 | solution.py:126
  80.3 4.8 collective-permute-start
  90.0 12.9 %conditional.8 = (bf16[128,1024]{1,0:T(8,128)(2,1)S(1)}, bf16[4,128,2048]{2,1,0:T(8,128)(2,1)}, bf16[4,128,2048]{2,1,0:T(8,128)(2,1)}, bf16[4,128,1024]{2,1,0:T(8,128)(2,1)}) conditional(s32[]{:T(128)} %convert_element_type.440, (bf16[4,128,2048]{2,1,0:T(8,128)(2,1)}, bf16[4,128,2048]{2,1,0:T(8,128)(2,1)}, ...), branch_computations={%region_1.1_spmd, %region_2.6_spmd} | conditional | flops 2157707264 | bytes 80231088 | solution.py:126
  112.3 17.3 %collective-permute-start = (bf16[128,1024]{1,0:T(8,128)(2,1)S(1)}, bf16[128,1024]{1,0:T(8,128)(2,1)S(1)}, u32[]{:S(2)}, u32[]{:S(2)}) collective-permute-start(bf16[128,1024]{1,0:T(8,128)(2,1)S(1)} %get-tuple-element.965), channel_id=1, source_target_pairs={{16,0},{32,16},{48,32},{64,48},{80,64},{96,80},{112,96},{17,1},{33... | collective-permute-start | bytes 786440 | tf_op jit(solution)/shard_map/while/body/eval_jaxpr/ppermute | solution.py:24
  143.5 54.4 %collective-permute-start = (bf16[128,1024]{1,0:T(8,128)(2,1)S(1)}, bf16[128,1024]{1,0:T(8,128)(2,1)S(1)}, u32[]{:S(2)}, u32[]{:S(2)}) collective-permute-start(bf16[128,1024]{1,0:T(8,128)(2,1)S(1)} %get-tuple-element.965), channel_id=1, source_target_pairs={{16,0},{32,16},{48,32},{64,48},{80,64},{96,80},{112,96},{17,1},{33... | collective-permute-start | bytes 786440 | tf_op jit(solution)/shard_map/while/body/eval_jaxpr/ppermute | solution.py:24
  201.2 12.9 %conditional.9 = (bf16[128,1024]{1,0:T(8,128)(2,1)S(1)}, bf16[4,128,2048]{2,1,0:T(8,128)(2,1)}, bf16[4,128,2048]{2,1,0:T(8,128)(2,1)}, bf16[4,128,1024]{2,1,0:T(8,128)(2,1)}) conditional(s32[]{:T(128)} %convert_element_type.441, (bf16[4,128,2048]{2,1,0:T(8,128)(2,1)}, bf16[4,128,2048]{2,1,0:T(8,128)(2,1)}, ...), branch_computations={%region_7.7_spmd, %region_8.12_spmd} | conditional | flops 2157707264 | bytes 80231088 | solution.py:126
  215.5 7.6 %collective-permute-start = (bf16[128,1024]{1,0:T(8,128)(2,1)S(1)}, bf16[128,1024]{1,0:T(8,128)(2,1)S(1)}, u32[]{:S(2)}, u32[]{:S(2)}) collective-permute-start(bf16[128,1024]{1,0:T(8,128)(2,1)S(1)} %get-tuple-element.965), channel_id=1, source_target_pairs={{16,0},{32,16},{48,32},{64,48},{80,64},{96,80},{112,96},{17,1},{33... | collective-permute-start | bytes 786440 | tf_op jit(solution)/shard_map/while/body/eval_jaxpr/ppermute | solution.py:24
  226.4 12.9 %conditional.9 = (bf16[128,1024]{1,0:T(8,128)(2,1)S(1)}, bf16[4,128,2048]{2,1,0:T(8,128)(2,1)}, bf16[4,128,2048]{2,1,0:T(8,128)(2,1)}, bf16[4,128,1024]{2,1,0:T(8,128)(2,1)}) conditional(s32[]{:T(128)} %convert_element_type.441, (bf16[4,128,2048]{2,1,0:T(8,128)(2,1)}, bf16[4,128,2048]{2,1,0:T(8,128)(2,1)}, ...), branch_computations={%region_7.7_spmd, %region_8.12_spmd} | conditional | flops 2157707264 | bytes 80231088 | solution.py:126
  240.6 20.7 %collective-permute-start = (bf16[128,1024]{1,0:T(8,128)(2,1)S(1)}, bf16[128,1024]{1,0:T(8,128)(2,1)S(1)}, u32[]{:S(2)}, u32[]{:S(2)}) collective-permute-start(bf16[128,1024]{1,0:T(8,128)(2,1)S(1)} %get-tuple-element.965), channel_id=1, source_target_pairs={{16,0},{32,16},{48,32},{64,48},{80,64},{96,80},{112,96},{17,1},{33... | collective-permute-start | bytes 786440 | tf_op jit(solution)/shard_map/while/body/eval_jaxpr/ppermute | solution.py:24
  264.7 12.8 %conditional.9 = (bf16[128,1024]{1,0:T(8,128)(2,1)S(1)}, bf16[4,128,2048]{2,1,0:T(8,128)(2,1)}, bf16[4,128,2048]{2,1,0:T(8,128)(2,1)}, bf16[4,128,1024]{2,1,0:T(8,128)(2,1)}) conditional(s32[]{:T(128)} %convert_element_type.441, (bf16[4,128,2048]{2,1,0:T(8,128)(2,1)}, bf16[4,128,2048]{2,1,0:T(8,128)(2,1)}, ...), branch_computations={%region_7.7_spmd, %region_8.12_spmd} | conditional | flops 2157707264 | bytes 80231088 | solution.py:126
  278.9 8.1 %collective-permute-start = (bf16[128,1024]{1,0:T(8,128)(2,1)S(1)}, bf16[128,1024]{1,0:T(8,128)(2,1)S(1)}, u32[]{:S(2)}, u32[]{:S(2)}) collective-permute-start(bf16[128,1024]{1,0:T(8,128)(2,1)S(1)} %get-tuple-element.965), channel_id=1, source_target_pairs={{16,0},{32,16},{48,32},{64,48},{80,64},{96,80},{112,96},{17,1},{33... | collective-permute-start | bytes 786440 | tf_op jit(solution)/shard_map/while/body/eval_jaxpr/ppermute | solution.py:24
  290.3 6.2 bitcast_convert_fusion.1
  296.5 11.2 %conditional.5 = ((bf16[4,128,2048]{2,1,0:T(8,128)(2,1)}, bf16[4,128,2048]{2,1,0:T(8,128)(2,1)}, bf16[4,128,1024]{2,1,0:T(8,128)(2,1)})) conditional(s32[]{:T(128)} %convert_element_type.243, (bf16[4,128,2048]{2,1,0:T(8,128)(2,1)}, bf16[4,128,2048]{2,1,0:T(8,128)(2,1)}, bf16[4,128,1024]{2,1,0:T(8,128)(2,1)}) %tuple.71, (s32[]{:T(128)}, ...), branch_computations={%region_20.21_spmd, %region_21.26_spmd} | conditional | flops 1619656832 | bytes 48771704 | solution.py:126
  307.7 6.3 bitcast_convert_fusion
  314.0 8.4 %pad_maximum_fusion.1 = bf16[2048,2048]{0,1:T(8,128)(2,1)} fusion(bf16[2048,1024]{0,1:T(8,128)(2,1)} %bitcast_convert_fusion, bf16[2048,1024]{0,1:T(8,128)(2,1)} %bitcast_convert_fusion.1), kind=kLoop, calls=%fused_computation.167 | loop fusion | flops 16777216 | bytes 16777216 | tf_op jit(solution)/shard_map/concatenate | solution.py:153
  322.4 12.3 %copy.35 = bf16[2048,2048]{1,0:T(8,128)(2,1)} copy(bf16[2048,2048]{0,1:T(8,128)(2,1)} %pad_maximum_fusion.1) | data formatting | bytes 16777216
  345.3 7.8 %pad_maximum_fusion = bf16[1024,4096]{1,0:T(8,128)(2,1)} fusion(bf16[1024,2048]{1,0:T(8,128)(2,1)} %bitcast_convert_fusion.2, bf16[1024,2048]{1,0:T(8,128)(2,1)} %bitcast_convert_fusion.3), kind=kLoop, calls=%fused_computation.166 | loop fusion | flops 16777216 | bytes 16777216 | tf_op jit(solution)/shard_map/concatenate | solution.py:149
  362.8 104.3 %reduce-scatter.7.cloned.1.call-done = bf16[128,2048]{1,0:T(8,128)(2,1)} async-done(((bf16[2048,2048]{1,0:T(8,128)(2,1)}), bf16[128,2048]{1,0:T(8,128)(2,1)}) %reduce-scatter.7.cloned.1.call-update) | async-done | bytes 524304
  470.0 96.0 %reduce-scatter.5.cloned.1.call-done = bf16[64,4096]{1,0:T(8,128)(2,1)} async-done(((bf16[1024,4096]{1,0:T(8,128)(2,1)}), bf16[64,4096]{1,0:T(8,128)(2,1)}) %reduce-scatter.5.cloned.1.call-update) | async-done | bytes 524304 | tf_op jit(solution)/shard_map/reduce_scatter | solution.py:148
  608.2 5.6 collective-permute-done.10
  (311 shorter events, 248.3 us)
Async XLA Ops:
  7.2 460.0 %reduce-scatter.7.cloned.1.call-start = ((), (), s32[]{:S(2)}) async-start(), calls=%async_computation.3 | async-start | bytes 8912896
  21.9 15.5 %collective-permute-start.1 = (bf16[128,1024]{1,0:T(8,128)(2,1)S(1)}, bf16[128,1024]{1,0:T(8,128)(2,1)S(1)}, u32[]{:S(2)}, u32[]{:S(2)}) collective-permute-start(bf16[128,1024]{1,0:T(8,128)(2,1)S(1)} %get-tuple-element.966), channel_id=1, source_target_pairs={{0,16},{16,32},{32,48},{48,64},{64,80},{80,96},{96,112},{1,17},{17... | collective-permute-start | bytes 786440 | tf_op jit(solution)/shard_map/while/body/eval_jaxpr/ppermute | solution.py:24
  42.7 19.0 %collective-permute-start.1 = (bf16[128,1024]{1,0:T(8,128)(2,1)S(1)}, bf16[128,1024]{1,0:T(8,128)(2,1)S(1)}, u32[]{:S(2)}, u32[]{:S(2)}) collective-permute-start(bf16[128,1024]{1,0:T(8,128)(2,1)S(1)} %get-tuple-element.966), channel_id=1, source_target_pairs={{0,16},{16,32},{32,48},{48,64},{64,80},{80,96},{96,112},{1,17},{17... | collective-permute-start | bytes 786440 | tf_op jit(solution)/shard_map/while/body/eval_jaxpr/ppermute | solution.py:24
  66.1 19.0 %collective-permute-start.1 = (bf16[128,1024]{1,0:T(8,128)(2,1)S(1)}, bf16[128,1024]{1,0:T(8,128)(2,1)S(1)}, u32[]{:S(2)}, u32[]{:S(2)}) collective-permute-start(bf16[128,1024]{1,0:T(8,128)(2,1)S(1)} %get-tuple-element.966), channel_id=1, source_target_pairs={{0,16},{16,32},{32,48},{48,64},{64,80},{80,96},{96,112},{1,17},{17... | collective-permute-start | bytes 786440 | tf_op jit(solution)/shard_map/while/body/eval_jaxpr/ppermute | solution.py:24
  88.7 19.0 %collective-permute-start.1 = (bf16[128,1024]{1,0:T(8,128)(2,1)S(1)}, bf16[128,1024]{1,0:T(8,128)(2,1)S(1)}, u32[]{:S(2)}, u32[]{:S(2)}) collective-permute-start(bf16[128,1024]{1,0:T(8,128)(2,1)S(1)} %get-tuple-element.966), channel_id=1, source_target_pairs={{0,16},{16,32},{32,48},{48,64},{64,80},{80,96},{96,112},{1,17},{17... | collective-permute-start | bytes 786440 | tf_op jit(solution)/shard_map/while/body/eval_jaxpr/ppermute | solution.py:24
  111.0 18.7 %collective-permute-start.1 = (bf16[128,1024]{1,0:T(8,128)(2,1)S(1)}, bf16[128,1024]{1,0:T(8,128)(2,1)S(1)}, u32[]{:S(2)}, u32[]{:S(2)}) collective-permute-start(bf16[128,1024]{1,0:T(8,128)(2,1)S(1)} %get-tuple-element.966), channel_id=1, source_target_pairs={{0,16},{16,32},{32,48},{48,64},{64,80},{80,96},{96,112},{1,17},{17... | collective-permute-start | bytes 786440 | tf_op jit(solution)/shard_map/while/body/eval_jaxpr/ppermute | solution.py:24
  112.3 20.6 %collective-permute-start = (bf16[128,1024]{1,0:T(8,128)(2,1)S(1)}, bf16[128,1024]{1,0:T(8,128)(2,1)S(1)}, u32[]{:S(2)}, u32[]{:S(2)}) collective-permute-start(bf16[128,1024]{1,0:T(8,128)(2,1)S(1)} %get-tuple-element.965), channel_id=1, source_target_pairs={{16,0},{32,16},{48,32},{64,48},{80,64},{96,80},{112,96},{17,1},{33... | collective-permute-start | bytes 786440 | tf_op jit(solution)/shard_map/while/body/eval_jaxpr/ppermute | solution.py:24
  142.2 57.5 %collective-permute-start.1 = (bf16[128,1024]{1,0:T(8,128)(2,1)S(1)}, bf16[128,1024]{1,0:T(8,128)(2,1)S(1)}, u32[]{:S(2)}, u32[]{:S(2)}) collective-permute-start(bf16[128,1024]{1,0:T(8,128)(2,1)S(1)} %get-tuple-element.966), channel_id=1, source_target_pairs={{0,16},{16,32},{32,48},{48,64},{64,80},{80,96},{96,112},{1,17},{17... | collective-permute-start | bytes 786440 | tf_op jit(solution)/shard_map/while/body/eval_jaxpr/ppermute | solution.py:24
  143.5 57.7 %collective-permute-start = (bf16[128,1024]{1,0:T(8,128)(2,1)S(1)}, bf16[128,1024]{1,0:T(8,128)(2,1)S(1)}, u32[]{:S(2)}, u32[]{:S(2)}) collective-permute-start(bf16[128,1024]{1,0:T(8,128)(2,1)S(1)} %get-tuple-element.965), channel_id=1, source_target_pairs={{16,0},{32,16},{48,32},{64,48},{80,64},{96,80},{112,96},{17,1},{33... | collective-permute-start | bytes 786440 | tf_op jit(solution)/shard_map/while/body/eval_jaxpr/ppermute | solution.py:24
  239.3 23.9 %collective-permute-start.1 = (bf16[128,1024]{1,0:T(8,128)(2,1)S(1)}, bf16[128,1024]{1,0:T(8,128)(2,1)S(1)}, u32[]{:S(2)}, u32[]{:S(2)}) collective-permute-start(bf16[128,1024]{1,0:T(8,128)(2,1)S(1)} %get-tuple-element.966), channel_id=1, source_target_pairs={{0,16},{16,32},{32,48},{48,64},{64,80},{80,96},{96,112},{1,17},{17... | collective-permute-start | bytes 786440 | tf_op jit(solution)/shard_map/while/body/eval_jaxpr/ppermute | solution.py:24
  240.6 24.0 %collective-permute-start = (bf16[128,1024]{1,0:T(8,128)(2,1)S(1)}, bf16[128,1024]{1,0:T(8,128)(2,1)S(1)}, u32[]{:S(2)}, u32[]{:S(2)}) collective-permute-start(bf16[128,1024]{1,0:T(8,128)(2,1)S(1)} %get-tuple-element.965), channel_id=1, source_target_pairs={{16,0},{32,16},{48,32},{64,48},{80,64},{96,80},{112,96},{17,1},{33... | collective-permute-start | bytes 786440 | tf_op jit(solution)/shard_map/while/body/eval_jaxpr/ppermute | solution.py:24
  334.7 231.3 %reduce-scatter.5.cloned.1.call-start = ((), (), s32[]{:S(2)}) async-start(), calls=%async_computation.2 | async-start | bytes 8912896 | tf_op jit(solution)/shard_map/reduce_scatter | solution.py:148
  359.9 207.9 %collective-permute-start.15 = (bf16[128,1024]{0,1:T(8,128)(2,1)}, bf16[128,1024]{0,1:T(8,128)(2,1)}, u32[]{:S(2)}, u32[]{:S(2)}) collective-permute-start(bf16[128,1024]{0,1:T(8,128)(2,1)} %collective-permute-done.14), channel_id=1, source_target_pairs={{0,32},{16,48},{32,0},{48,16},{64,96},{80,112},{96,64},{112,80},{1... | collective-permute-start | bytes 786440 | tf_op jit(solution)/shard_map/ppermute | solution.py:28
  362.7 209.1 %collective-permute-start.6 = (bf16[64,2048]{1,0:T(8,128)(2,1)}, bf16[64,2048]{1,0:T(8,128)(2,1)S(1)}, u32[]{:S(2)}, u32[]{:S(2)}) collective-permute-start(bf16[64,2048]{1,0:T(8,128)(2,1)} %collective-permute-done.5), channel_id=1, source_target_pairs={{0,32},{16,48},{32,0},{48,16},{64,96},{80,112},{96,64},{112,80},{1... | collective-permute-start | bytes 786440 | tf_op jit(solution)/shard_map/ppermute | solution.py:28
  468.5 100.2 %collective-permute-start.11 = (bf16[128,1024]{0,1:T(8,128)(2,1)S(1)}, bf16[128,1024]{0,1:T(8,128)(2,1)}, u32[]{:S(2)}, u32[]{:S(2)}) collective-permute-start(bf16[128,1024]{0,1:T(8,128)(2,1)S(1)} %get-tuple-element.840), channel_id=1, source_target_pairs={{0,16},{16,0},{32,48},{48,32},{64,80},{80,64},{96,112},{112,96},{1... | collective-permute-start | bytes 786440 | tf_op jit(solution)/shard_map/ppermute | solution.py:28
  469.1 100.7 %collective-permute-start.17 = (bf16[128,1024]{0,1:T(8,128)(2,1)S(1)}, bf16[128,1024]{0,1:T(8,128)(2,1)}, u32[]{:S(2)}, u32[]{:S(2)}) collective-permute-start(bf16[128,1024]{0,1:T(8,128)(2,1)S(1)} %get-tuple-element.841), channel_id=1, source_target_pairs={{0,16},{16,0},{32,48},{48,32},{64,80},{80,64},{96,112},{112,96},{1... | collective-permute-start | bytes 786440 | tf_op jit(solution)/shard_map/ppermute | solution.py:28
  568.7 18.1 %collective-permute-start.12 = (bf16[128,1024]{0,1:T(8,128)(2,1)}, bf16[128,1024]{0,1:T(8,128)(2,1)}, u32[]{:S(2)}, u32[]{:S(2)}) collective-permute-start(bf16[128,1024]{0,1:T(8,128)(2,1)} %collective-permute-done.11), channel_id=1, source_target_pairs={{0,32},{16,48},{32,0},{48,16},{64,96},{80,112},{96,64},{112,80},{1... | collective-permute-start | bytes 786440 | tf_op jit(solution)/shard_map/ppermute | solution.py:28
  569.9 22.6 %collective-permute-start.18 = (bf16[128,1024]{0,1:T(8,128)(2,1)}, bf16[128,1024]{0,1:T(8,128)(2,1)}, u32[]{:S(2)}, u32[]{:S(2)}) collective-permute-start(bf16[128,1024]{0,1:T(8,128)(2,1)} %collective-permute-done.17), channel_id=1, source_target_pairs={{0,32},{16,48},{32,0},{48,16},{64,96},{80,112},{96,64},{112,80},{1... | collective-permute-start | bytes 786440 | tf_op jit(solution)/shard_map/ppermute | solution.py:28
  571.7 23.2 %collective-permute-start.16 = (bf16[128,1024]{0,1:T(8,128)(2,1)}, bf16[128,1024]{0,1:T(8,128)(2,1)}, u32[]{:S(2)}, u32[]{:S(2)}) collective-permute-start(bf16[128,1024]{0,1:T(8,128)(2,1)} %collective-permute-done.15), channel_id=1, source_target_pairs={{0,64},{16,80},{32,96},{48,112},{64,0},{80,16},{96,32},{112,48},{1... | collective-permute-start | bytes 786440 | tf_op jit(solution)/shard_map/ppermute | solution.py:28
  575.7 22.4 %collective-permute-start.9 = (bf16[64,2048]{1,0:T(8,128)(2,1)}, bf16[64,2048]{1,0:T(8,128)(2,1)}, u32[]{:S(2)}, u32[]{:S(2)}) collective-permute-start(bf16[64,2048]{1,0:T(8,128)(2,1)} %collective-permute-done.8), channel_id=1, source_target_pairs={{0,32},{16,48},{32,0},{48,16},{64,96},{80,112},{96,64},{112,80},{1... | collective-permute-start | bytes 786440 | tf_op jit(solution)/shard_map/ppermute | solution.py:28
  581.3 21.5 %collective-permute-start.3 = (bf16[64,2048]{1,0:T(8,128)(2,1)}, bf16[64,2048]{1,0:T(8,128)(2,1)}, u32[]{:S(2)}, u32[]{:S(2)}) collective-permute-start(bf16[64,2048]{1,0:T(8,128)(2,1)} %collective-permute-done.2), channel_id=1, source_target_pairs={{0,32},{16,48},{32,0},{48,16},{64,96},{80,112},{96,64},{112,80},{1... | collective-permute-start | bytes 786440 | tf_op jit(solution)/shard_map/ppermute | solution.py:28
  586.9 16.6 %collective-permute-start.13 = (bf16[128,1024]{0,1:T(8,128)(2,1)}, bf16[128,1024]{0,1:T(8,128)(2,1)}, u32[]{:S(2)}, u32[]{:S(2)}) collective-permute-start(bf16[128,1024]{0,1:T(8,128)(2,1)} %collective-permute-done.12), channel_id=1, source_target_pairs={{0,64},{16,80},{32,96},{48,112},{64,0},{80,16},{96,32},{112,48},{1... | collective-permute-start | bytes 786440 | tf_op jit(solution)/shard_map/ppermute | solution.py:28
  598.1 15.8 %collective-permute-start.10 = (bf16[64,2048]{1,0:T(8,128)(2,1)}, bf16[64,2048]{1,0:T(8,128)(2,1)}, u32[]{:S(2)}, u32[]{:S(2)}) collective-permute-start(bf16[64,2048]{1,0:T(8,128)(2,1)} %collective-permute-done.9), channel_id=1, source_target_pairs={{0,64},{16,80},{32,96},{48,112},{64,0},{80,16},{96,32},{112,48},{1... | collective-permute-start | bytes 786440 | tf_op jit(solution)/shard_map/ppermute | solution.py:28
  602.9 15.7 %collective-permute-start.4 = (bf16[64,2048]{1,0:T(8,128)(2,1)}, bf16[64,2048]{1,0:T(8,128)(2,1)}, u32[]{:S(2)}, u32[]{:S(2)}) collective-permute-start(bf16[64,2048]{1,0:T(8,128)(2,1)} %collective-permute-done.3), channel_id=1, source_target_pairs={{0,64},{16,80},{32,96},{48,112},{64,0},{80,16},{96,32},{112,48},{1... | collective-permute-start | bytes 786440 | tf_op jit(solution)/shard_map/ppermute | solution.py:28
  (55 other events, 409.9 us)
Sparse Core Ops, SparseCore 0:
  334.8 132.2 reduce-scatter.6
  469.5 96.4 reduce-scatter.4
where the time goes:
time: 633 us; the launch traced here: 628 us
  waiting for transfers between devices  276 us (44%)
  starting transfers between devices  158 us (25%)
  matrix products  110 us (17%)
  local copies, waits for them, and re-layouts  36 us (6%)
  other arithmetic  32.8 us (5%)
  between operations  14.3 us (2%)
    ppermute x20, starting transfers between devices, from_behind(): lax.ppermute(value, axis, [(source, source + steps) for source in range(l...  141 us
    unnamed x3, waiting for transfers between devices  104 us
    reduce_scatter x1, waiting for transfers between devices, on_device(): lax.psum_scatter(jnp.concatenate(parts, axis=1).astype(jnp.bfloat16), 'dp...  96 us
    ppermute x18, waiting for transfers between devices, partner(): lax.ppermute(x, axis, [(i, i ^ 1 << bit) for i in range(lax.axis_size(axi...  39.7 us
    ppermute x20, waiting for transfers between devices, from_behind(): lax.ppermute(value, axis, [(source, source + steps) for source in range(l...  36 us
    dot_general x8, matrix products, local_backward(): preact = jnp.dot(inputs, w_up, preferred_element_type=jnp.float32)  32.5 us
    dot_general x15, matrix products, times_transpose(): lax.dot_general(left, right, (((1,), (1,)), ((), ())), preferred_element_...  30.7 us
    dot_general x8, matrix products, local_backward(): jnp.dot(hidden, w_down, preferred_element_type=jnp.float32)  25.9 us
  transfers between devices with their start and end apart: 40, of which 28 were waited for; matrix products, arithmetic and copies ran while one was open for 12% of the time, Pallas kernels for 0%

commit v1 on v0

v1 whole, which is shorter than its diff:
```python
import functools

import jax
import jax.numpy as jnp
from jax import lax
from jax.experimental import pallas as pl
from jax.experimental.pallas import tpu as pltpu
from jax.sharding import PartitionSpec as P

norm_epsilon = 1e-06
momentum_decay = 0.9
step_size = 0.01
root_half = 0.7071067811865476
inv_root_tau = 0.3989422804014327
MESH = pl.DeviceIdType.MESH
bf16 = jnp.bfloat16
f32 = jnp.float32


def times_transpose(left, right):
    return lax.dot_general(
        left, right, (((1,), (1,)), ((), ())), preferred_element_type=f32
    )


def contract_rows(left, right):
    return lax.dot_general(
        left, right, (((0,), (0,)), ((), ())), preferred_element_type=f32
    )


def relay_kernel(
    sections, micro, rows, model, width, tile, ahead,
    inputs_hbm, top_hbm, up_hbm, down_hbm,
    up_out, down_out,
    w_up, w_down, x_buf, hidden, slope, normed, scale_buf, grad_pre, grad_low, e_buf, sent,
    w_sem, own_sem, swap_send, swap_recv, top_send, e_recv, e_send,
):
    section = lax.axis_index("section")
    replica = lax.axis_index("dp")
    core = lax.rem(replica, 2)
    other = replica + 1 - 2 * core
    position = jnp.where(core == 0, sections - 1 - section, section)
    step_to = 2 * core - 1
    after = lax.rem(section + step_to + sections, sections)
    before = lax.rem(section - step_to + sections, sections)
    chunks = 2 * micro
    last = sections - 1

    w_up_copy = pltpu.make_async_copy(up_hbm.at[core, 0], w_up, w_sem.at[0])
    w_down_copy = pltpu.make_async_copy(down_hbm.at[core, 0], w_down, w_sem.at[1])

    def own_copy(slot):
        return pltpu.make_async_copy(
            inputs_hbm.at[core, slot], x_buf.at[2 * slot + core], own_sem.at[slot]
        )

    def swap_copy(slot):
        return pltpu.make_async_remote_copy(
            src_ref=inputs_hbm.at[1 - core, slot],
            dst_ref=x_buf.at[2 * slot + core],
            send_sem=swap_send.at[slot],
            recv_sem=swap_recv.at[slot],
            device_id=(section, other),
            device_id_type=MESH,
        )

    def top_own(slot):
        return pltpu.make_async_copy(
            top_hbm.at[core, slot], e_buf.at[2 * slot + core], e_recv.at[2 * slot + core]
        )

    def top_swap(slot):
        return pltpu.make_async_remote_copy(
            src_ref=top_hbm.at[1 - core, slot],
            dst_ref=e_buf.at[2 * slot + core],
            send_sem=top_send.at[slot],
            recv_sem=e_recv.at[2 * slot + core],
            device_id=(section, other),
            device_id_type=MESH,
        )

    def relay_copy(chunk):
        return pltpu.make_async_remote_copy(
            src_ref=sent.at[chunk],
            dst_ref=e_buf.at[chunk],
            send_sem=e_send.at[chunk],
            recv_sem=e_recv.at[chunk],
            device_id=(after, replica),
            device_id_type=MESH,
        )

    w_up_copy.start()
    for slot in range(micro):
        own_copy(slot).start()
    w_down_copy.start()

    barrier = pltpu.get_barrier_semaphore()
    pl.semaphore_signal(barrier, inc=1, device_id=(after, replica), device_id_type=MESH)
    pl.semaphore_signal(barrier, inc=1, device_id=(before, replica), device_id_type=MESH)
    pl.semaphore_signal(barrier, inc=1, device_id=(section, other), device_id_type=MESH)
    pl.semaphore_wait(barrier, 3)

    @pl.when(position == last)
    def _():
        for slot in range(micro):
            top_swap(slot).start()

    for slot in range(micro):
        swap_copy(slot).start()

    @pl.when(position == 0)
    def _():
        for slot in range(micro):
            top_own(slot).start()

    w_up_copy.wait()
    for slot in range(micro):
        own_copy(slot).wait()
        swap_copy(slot).wait()
    w_down_copy.wait()

    def forward(chunk):
        x = x_buf[chunk]

        for n in range(width // tile):
            cols = pl.ds(n * tile, tile)
            preact = jnp.dot(x, w_up[:, cols], preferred_element_type=f32)
            cdf = 0.5 * (1.0 + lax.erf(preact * root_half))
            hidden[chunk, :, cols] = (preact * cdf).astype(bf16)
            slope[chunk, :, cols] = cdf + preact * jnp.exp(-0.5 * preact * preact) * inv_root_tau
        summed = x.astype(f32) + jnp.dot(hidden[chunk], w_down[...], preferred_element_type=f32)
        centre = summed - jnp.mean(summed, axis=-1, keepdims=True)
        scale_inv = lax.rsqrt(jnp.mean(centre * centre, axis=-1, keepdims=True) + norm_epsilon)
        normed[chunk] = centre * scale_inv
        scale_buf[chunk] = jnp.broadcast_to(scale_inv, (rows, 128))

    def backward(chunk):
        pltpu.make_async_copy(sent.at[chunk], e_buf.at[chunk], e_recv.at[chunk]).wait()
        upstream = e_buf[chunk].astype(f32)
        y = normed[chunk]
        scale_inv = scale_buf[chunk][:, :1]
        grad_sum = scale_inv * (
            upstream
            - jnp.mean(upstream, axis=-1, keepdims=True)
            - y * jnp.mean(upstream * y, axis=-1, keepdims=True)
        )
        low = grad_sum.astype(bf16)
        grad_low[pl.ds(pl.multiple_of(chunk * rows, rows), rows), :] = low
        place = pl.ds(pl.multiple_of(chunk * rows, rows), rows)
        for n in range(width // tile):
            cols = pl.ds(n * tile, tile)
            grad = times_transpose(low, w_down[cols, :]) * slope[chunk, :, cols]
            grad_pre[place, cols] = grad.astype(bf16)

        @pl.when(position < last)
        def _():
            sent[chunk] = (grad_sum + times_transpose(grad_pre[place, :], w_up[...])).astype(bf16)
            relay_copy(chunk).start()

    lead = jnp.minimum(chunks, ahead * position)

    @pl.loop(0, 2 * chunks)
    def _(step):
        @pl.when(step < chunks)
        def _():
            forward(step)

        back = step - lead

        @pl.when(jnp.logical_and(back >= 0, back < chunks))
        def _():
            backward(back)

    total = chunks * rows
    span = 256 if model % 256 == 0 else 128

    @pl.loop(0, model // span)
    def _(t):
        cols = pl.ds(pl.multiple_of(t * span, span), span)
        left = x_buf[:, :, cols].reshape(total, span)
        up_out[cols, :] = contract_rows(left, grad_pre[...]).astype(bf16)

    @pl.loop(0, width // span)
    def _(t):
        cols = pl.ds(pl.multiple_of(t * span, span), span)
        left = hidden[:, :, cols].reshape(total, span)
        down_out[cols, :] = contract_rows(left, grad_low[...]).astype(bf16)

    @pl.when(position < last)
    def _():
        for chunk in range(chunks):
            relay_copy(chunk).wait_send()

    @pl.when(position == last)
    def _():
        for slot in range(micro):
            top_swap(slot).wait_send()


def relay(sections, ordered, top_grad, up_weight, down_weight):
    micro, rows, model = ordered.shape[1:]
    width = up_weight.shape[3]
    chunks = 2 * micro
    total = chunks * rows
    dma = pltpu.SemaphoreType.DMA
    flops = 2 * 6 * total * model * width
    return pl.pallas_call(
        functools.partial(relay_kernel, sections, micro, rows, model, width, min(512, width), 3),
        out_shape=[
            jax.ShapeDtypeStruct((model, width), bf16),
            jax.ShapeDtypeStruct((width, model), bf16),
        ],
        in_specs=[pl.BlockSpec(memory_space=pl.ANY)] * 4,
        out_specs=[pl.BlockSpec(memory_space=pltpu.VMEM)] * 2,
        scratch_shapes=[
            pltpu.VMEM((model, width), bf16),
            pltpu.VMEM((width, model), bf16),
            pltpu.VMEM((chunks, rows, model), bf16),
            pltpu.VMEM((chunks, rows, width), bf16),
            pltpu.VMEM((chunks, rows, width), f32),
            pltpu.VMEM((chunks, rows, model), f32),
            pltpu.VMEM((chunks, rows, 128), f32),
            pltpu.VMEM((total, width), bf16),
            pltpu.VMEM((total, model), bf16),
            pltpu.VMEM((chunks, rows, model), bf16),
            pltpu.VMEM((chunks, rows, model), bf16),
            dma((2,)),
            dma((micro,)),
            dma((micro,)),
            dma((micro,)),
            dma((micro,)),
            dma((chunks,)),
            dma((chunks,)),
        ],
        compiler_params=pltpu.CompilerParams(
            collective_id=0, has_side_effects=True, vmem_limit_bytes=60 * 1024 * 1024
        ),
        cost_estimate=pl.CostEstimate(flops=flops, bytes_accessed=24 << 20, transcendentals=0),
    )(ordered, top_grad, up_weight, down_weight)


def on_device(section_inputs, top_grad, plan, up_weight, down_weight, up_moment, down_moment):
    sections = lax.axis_size("section")
    replicas = lax.axis_size("dp")
    replica = lax.axis_index("dp")
    core = lax.rem(replica, 2)
    mirror = [(i, sections - 1 - i) for i in range(sections)]
    swap = [(i, i ^ 1) for i in range(replicas)]
    their_moment_up = lax.ppermute(up_moment[0].astype(bf16), "section", mirror)
    their_moment_down = lax.ppermute(down_moment[0].astype(bf16), "section", mirror)
    ordered = jnp.stack([section_inputs[c, 0][plan[c]] for c in range(2)])
    part_up, part_down = relay(sections, ordered, top_grad, up_weight, down_weight)
    groups = [list(range(0, replicas, 2)), list(range(1, replicas, 2))]

    def reduced(part):
        held = lax.psum_scatter(
            part, "dp", scatter_dimension=0, axis_index_groups=groups, tiled=True
        )
        half = held.shape[0] // 2
        mine = lax.dynamic_slice_in_dim(held, core * half, half, 0)
        give = lax.dynamic_slice_in_dim(held, (1 - core) * half, half, 0)
        got = lax.ppermute(give, "dp", swap)
        return jnp.where(core == 0, mine, got), jnp.where(core == 0, got, mine)

    own_up, far_up = reduced(part_up)
    own_down, far_down = reduced(part_down)
    their = [lax.ppermute(v, "section", mirror) for v in (own_up, far_up, own_down, far_down)]
    their_own_up, their_far_up, their_own_down, their_far_down = their

    def update(moment, their_moment, own, far, their_own, their_far, weights):
        rows = moment.shape[0]
        held = lax.dynamic_slice_in_dim(weights[:, 0], replica * rows, rows, 1).astype(f32)
        new = momentum_decay * moment + (own.astype(f32) + their_far.astype(f32))
        fresh = (held[0] - step_size * new).astype(bf16)
        mirrored = momentum_decay * their_moment.astype(f32) + (
            their_own.astype(f32) + far.astype(f32)
        )
        mirror_fresh = (held[1] - step_size * mirrored).astype(bf16)
        return new, jnp.stack([fresh, mirror_fresh])[:, None]

    moment_up, new_up = update(
        up_moment[0], their_moment_up, own_up, far_up, their_own_up, their_far_up, up_weight
    )
    moment_down, new_down = update(
        down_moment[0], their_moment_down, own_down, far_down,
        their_own_down, their_far_down, down_weight,
    )
    return (new_up, new_down, moment_up[None], moment_down[None])


def solution(mesh):
    in_specs = (
        P(None, "section", None, "dp", None),
        P(None, None, "dp", None),
        P(),
        P(None, "section", None, None),
        P(None, "section", None, None),
        P("section", "dp", None),
        P("section", "dp", None),
    )
    out_specs = (
        P(None, "section", "dp", None),
        P(None, "section", "dp", None),
        P("section", "dp", None),
        P("section", "dp", None),
    )
    return jax.shard_map(
        on_device, mesh=mesh, in_specs=in_specs, out_specs=out_specs, check_vma=False
    )
```

time: 633 us -> 367 us (0.58)
  starting transfers between devices: 158 us -> 13.8 us
  Pallas kernels: 0 us -> 115 us
  matrix products: 110 us -> 0 us
  waiting for transfers between devices: 276 us -> 199 us
  local copies, waits for them, and re-layouts: 36 us -> 6.7 us
  other arithmetic: 32.8 us -> 15.4 us
    ppermute x38 -> x8, starting transfers between devices: 157 us -> 13.8 us  [the longest x4 7.49 us: on_device(): lax.ppermute(v, 'section', mirror)]
    pallas_call x0 -> x1, Pallas kernels: none -> 115 us  [relay(): pl.pallas_call(functools.partial(relay_kernel, sections, micro, rows, mod...]
    dot_general x35 -> x0, matrix products: 110 us -> none  [the longest x8 32.5 us: local_backward(): preact = jnp.dot(inputs, w_up, preferred_element_type=jnp.float32)]
    unnamed x3 -> x2, waiting for transfers between devices: 104 us -> 0.69 us
    reduce_scatter x1 -> x2, waiting for transfers between devices: 96 us -> 182 us  [reduced(): lax.psum_scatter(part, 'dp', scatter_dimension=0, axis_index_groups=group...]
    ppermute x38 -> x8, waiting for transfers between devices: 75.8 us -> 16.4 us  [the longest x4 16.4 us: on_device(): lax.ppermute(v, 'section', mirror)]
    unnamed x25 -> x6, local copies, waits for them, and re-layouts: 19 us -> 0.36 us
    concatenate x2 -> x0, other arithmetic: 16.2 us -> none  [on_device(): jnp.concatenate(parts, axis=1).astype(jnp.bfloat16)]
  transfers between devices with their start and end apart: 40 -> 10, of which waited for: 28 -> 6; matrix products, arithmetic and copies ran while one was open for 12% -> 4% of each run, Pallas kernels for 0% -> 0%
where the time goes in v1:
time: 367 us; the launch traced here: 364 us
  waiting for transfers between devices  199 us (54%)
  Pallas kernels  115 us (31%)
  other arithmetic  15.4 us (4%)
  between operations  14.2 us (4%)
  starting transfers between devices  13.8 us (4%)
  local copies, waits for them, and re-layouts  6.7 us (2%)
    reduce_scatter x2, waiting for transfers between devices, reduced(): lax.psum_scatter(part, 'dp', scatter_dimension=0, axis_index_groups=group...  182 us
    pallas_call x1, Pallas kernels, relay(): pl.pallas_call(functools.partial(relay_kernel, sections, micro, rows, mod...  115 us
    ppermute x4, waiting for transfers between devices, on_device(): lax.ppermute(v, 'section', mirror)  16.4 us
    ppermute x4, starting transfers between devices, on_device(): lax.ppermute(v, 'section', mirror)  7.49 us
  transfers between devices with their start and end apart: 10, of which 6 were waited for; matrix products, arithmetic and copies ran while one was open for 4% of the time, Pallas kernels for 0%

profile of v1, /device:TPU:31, one launch (start us, length us, event | category | flops | bytes accessed | tf_op | source)
XLA Modules:
  0.0 364.2 jit_solution(15698046104875921844)
XLA Ops:
  8.0 1.8 slice_bitcast_fusion.1
  11.0 1.6 pad_maximum_fusion.inputs_hbm
  12.6 115.0 %shard_map.102 = (bf16[1024,2048]{1,0:T(8,128)(2,1)}, bf16[2048,1024]{1,0:T(8,128)(2,1)}) custom-call(bf16[2,4,128,1024]{3,2,1,0:T(8,128)(2,1)} %pad_maximum_fusion.inputs_hbm, bf16[2,4,128,1024]{3,2,1,0:T(8,128)(2,1)} %top_hbm.1, bf16[2,1,1024,2048]{3,2,1,0:T(8,128)(2,1)} %up_hbm.1, bf16[2,1,2048,1024]{3,2,1,0:T(8,128)(2,1)} %down_hbm.1), custom_call_target="tpu_custom_call" | custom-call | flops 25769803776 | bytes 25165824 | tf_op jit(solution)/shard_map/pallas_call | solution.py:208
  130.2 5.1 %collective-permute-start.2 = (bf16[64,2048]{1,0:T(8,128)(2,1)}, bf16[64,2048]{1,0:T(8,128)(2,1)}, u32[]{:S(2)}, u32[]{:S(2)}) collective-permute-start(bf16[64,2048]{1,0:T(8,128)(2,1)} %convert_bitcast_fusion.1), channel_id=1, source_target_pairs={{0,112},{16,96},{32,80},{48,64},{64,48},{80,32},{96,16},{112,0},{1... | collective-permute-start | bytes 786440 | tf_op jit(solution)/shard_map/ppermute | solution.py:250
  135.3 1.1 dynamic-slice_convert_fusion.1
  136.5 90.3 %reduce-scatter.5.cloned.1.call-done = bf16[256,1024]{1,0:T(8,128)(2,1)} async-done(((bf16[2048,1024]{1,0:T(8,128)(2,1)}), bf16[256,1024]{1,0:T(8,128)(2,1)}) %reduce-scatter.5.cloned.1.call-update) | async-done | bytes 524304 | tf_op jit(solution)/shard_map/reduce_scatter | solution.py:257
  226.7 1.7 constant_dynamic-slice_fusion
  228.8 91.8 %reduce-scatter.3.cloned.1.call-done = bf16[128,2048]{1,0:T(8,128)(2,1)} async-done(((bf16[1024,2048]{1,0:T(8,128)(2,1)}), bf16[128,2048]{1,0:T(8,128)(2,1)}) %reduce-scatter.3.cloned.1.call-update) | async-done | bytes 524304 | tf_op jit(solution)/shard_map/reduce_scatter | solution.py:257
  320.6 1.7 constant_dynamic-slice_fusion.1
  323.0 1.1 dynamic-slice_convert_fusion
  324.2 1.1 broadcast_select_fusion
  325.3 0.9 collective-permute-start.5
  326.2 1.0 broadcast_select_fusion.2
  327.2 4.4 %collective-permute-start.1 = (bf16[64,2048]{1,0:T(8,128)(2,1)S(1)}, bf16[64,2048]{1,0:T(8,128)(2,1)S(1)}, u32[]{:S(2)}, u32[]{:S(2)}) collective-permute-start(bf16[64,2048]{1,0:T(8,128)(2,1)S(1)} %broadcast_select_fusion.2), channel_id=1, source_target_pairs={{0,112},{16,96},{32,80},{48,64},{64,48},{80,32},{96,16},{112,0},{1... | collective-permute-start | bytes 786440 | tf_op jit(solution)/shard_map/ppermute | solution.py:268
  331.6 5.2 %collective-permute-done.5 = bf16[128,1024]{1,0:T(8,128)(2,1)S(1)} collective-permute-done((bf16[128,1024]{1,0:T(8,128)(2,1)S(1)}, bf16[128,1024]{1,0:T(8,128)(2,1)S(1)}, u32[]{:S(2)}, u32[]{:S(2)}) %collective-permute-start.5) | collective-permute-done | bytes 262176 | tf_op jit(solution)/shard_map/ppermute | solution.py:268
  336.8 2.0 fusion.13
  339.6 2.8 collective-permute-done.1
  342.4 0.9 fusion.12
  343.4 1.5 collective-permute-start.3
  344.8 4.1 %collective-permute-done.7 = bf16[128,1024]{1,0:T(8,128)(2,1)S(1)} collective-permute-done((bf16[128,1024]{1,0:T(8,128)(2,1)S(1)}, bf16[128,1024]{1,0:T(8,128)(2,1)S(1)}, u32[]{:S(2)}, u32[]{:S(2)}) %collective-permute-start.7) | collective-permute-done | bytes 262176 | tf_op jit(solution)/shard_map/ppermute | solution.py:268
  348.9 1.3 fusion.10
  351.0 4.3 %collective-permute-done.3 = bf16[64,2048]{1,0:T(8,128)(2,1)S(1)} collective-permute-done((bf16[64,2048]{1,0:T(8,128)(2,1)S(1)}, bf16[64,2048]{1,0:T(8,128)(2,1)S(1)}, u32[]{:S(2)}, u32[]{:S(2)}) %collective-permute-start.3) | collective-permute-done | bytes 262176 | tf_op jit(solution)/shard_map/ppermute | solution.py:268
  355.3 1.3 fusion.8
  356.6 0.8 maximum_bitcast_fusion
  (25 shorter events, 7.4 us)
Async XLA Ops:
  7.2 219.6 %reduce-scatter.5.cloned.1.call-start = ((), (), s32[]{:S(2)}) async-start(), calls=%async_computation.3 | async-start | bytes 4718592 | tf_op jit(solution)/shard_map/reduce_scatter | solution.py:257
  127.7 193.0 %reduce-scatter.3.cloned.1.call-start = ((), (), s32[]{:S(2)}) async-start(), calls=%async_computation.2 | async-start | bytes 4718592 | tf_op jit(solution)/shard_map/reduce_scatter | solution.py:257
  127.7 1.0 copy-start
  127.7 1.8 copy-start.1
  129.5 215.3 %collective-permute-start.6 = (bf16[128,1024]{1,0:T(8,128)(2,1)}, bf16[128,1024]{1,0:T(8,128)(2,1)}, u32[]{:S(2)}, u32[]{:S(2)}) collective-permute-start(bf16[128,1024]{1,0:T(8,128)(2,1)} %convert_bitcast_fusion), channel_id=1, source_target_pairs={{0,112},{16,96},{32,80},{48,64},{64,48},{80,32},{96,16},{112,0},{1... | collective-permute-start | bytes 786440 | tf_op jit(solution)/shard_map/ppermute | solution.py:251
  130.2 220.8 %collective-permute-start.2 = (bf16[64,2048]{1,0:T(8,128)(2,1)}, bf16[64,2048]{1,0:T(8,128)(2,1)}, u32[]{:S(2)}, u32[]{:S(2)}) collective-permute-start(bf16[64,2048]{1,0:T(8,128)(2,1)} %convert_bitcast_fusion.1), channel_id=1, source_target_pairs={{0,112},{16,96},{32,80},{48,64},{64,48},{80,32},{96,16},{112,0},{1... | collective-permute-start | bytes 786440 | tf_op jit(solution)/shard_map/ppermute | solution.py:250
  228.4 95.8 %collective-permute-start.4 = (bf16[128,1024]{1,0:T(8,128)(2,1)}, bf16[128,1024]{1,0:T(8,128)(2,1)}, u32[]{:S(2)}, u32[]{:S(2)}) collective-permute-start(bf16[128,1024]{1,0:T(8,128)(2,1)} %constant_dynamic-slice_fusion), channel_id=1, source_target_pairs={{0,1},{1,0},{2,3},{3,2},{4,5},{5,4},{6,7},{7,6},{8,9},{9,8},{10,11... | collective-permute-start | bytes 786440 | tf_op jit(solution)/shard_map/ppermute | solution.py:263
  322.3 3.9 %collective-permute-start = (bf16[64,2048]{1,0:T(8,128)(2,1)}, bf16[64,2048]{1,0:T(8,128)(2,1)S(1)}, u32[]{:S(2)}, u32[]{:S(2)}) collective-permute-start(bf16[64,2048]{1,0:T(8,128)(2,1)} %constant_dynamic-slice_fusion.1), channel_id=1, source_target_pairs={{0,1},{1,0},{2,3},{3,2},{4,5},{5,4},{6,7},{7,6},{8,9},{9,8},{10,11... | collective-permute-start | bytes 786440 | tf_op jit(solution)/shard_map/ppermute | solution.py:263
  324.2 18.2 %copy-start.2 = (bf16[128,2048]{1,0:T(8,128)(2,1)S(1)}, bf16[128,2048]{1,0:T(8,128)(2,1)}, u32[]{:S(2)}) copy-start(bf16[128,2048]{1,0:T(8,128)(2,1)} %reduce-scatter.3.cloned.1.call-done) | copy-start | bytes 1572868
  325.3 11.5 %collective-permute-start.5 = (bf16[128,1024]{1,0:T(8,128)(2,1)S(1)}, bf16[128,1024]{1,0:T(8,128)(2,1)S(1)}, u32[]{:S(2)}, u32[]{:S(2)}) collective-permute-start(bf16[128,1024]{1,0:T(8,128)(2,1)S(1)} %broadcast_select_fusion), channel_id=1, source_target_pairs={{0,112},{16,96},{32,80},{48,64},{64,48},{80,32},{96,16},{112,0},{1... | collective-permute-start | bytes 786440 | tf_op jit(solution)/shard_map/ppermute | solution.py:268
  327.2 15.2 %collective-permute-start.1 = (bf16[64,2048]{1,0:T(8,128)(2,1)S(1)}, bf16[64,2048]{1,0:T(8,128)(2,1)S(1)}, u32[]{:S(2)}, u32[]{:S(2)}) collective-permute-start(bf16[64,2048]{1,0:T(8,128)(2,1)S(1)} %broadcast_select_fusion.2), channel_id=1, source_target_pairs={{0,112},{16,96},{32,80},{48,64},{64,48},{80,32},{96,16},{112,0},{1... | collective-permute-start | bytes 786440 | tf_op jit(solution)/shard_map/ppermute | solution.py:268
  338.8 10.1 %collective-permute-start.7 = (bf16[128,1024]{1,0:T(8,128)(2,1)S(1)}, bf16[128,1024]{1,0:T(8,128)(2,1)S(1)}, u32[]{:S(2)}, u32[]{:S(2)}) collective-permute-start(bf16[128,1024]{1,0:T(8,128)(2,1)S(1)} %get-tuple-element.13), channel_id=1, source_target_pairs={{0,112},{16,96},{32,80},{48,64},{64,48},{80,32},{96,16},{112,0},{1... | collective-permute-start | bytes 786440 | tf_op jit(solution)/shard_map/ppermute | solution.py:268
  343.4 11.9 %collective-permute-start.3 = (bf16[64,2048]{1,0:T(8,128)(2,1)S(1)}, bf16[64,2048]{1,0:T(8,128)(2,1)S(1)}, u32[]{:S(2)}, u32[]{:S(2)}) collective-permute-start(bf16[64,2048]{1,0:T(8,128)(2,1)S(1)} %get-tuple-element.15), channel_id=1, source_target_pairs={{0,112},{16,96},{32,80},{48,64},{64,48},{80,32},{96,16},{112,0},{1... | collective-permute-start | bytes 786440 | tf_op jit(solution)/shard_map/ppermute | solution.py:268
Sparse Core Ops, SparseCore 0:
  127.8 98.8 reduce-scatter.4
  229.1 91.4 reduce-scatter.2

commit v2 on v1

v2 whole, which is shorter than its diff:
```python
import functools

import jax
import jax.numpy as jnp
from jax import lax
from jax.experimental import pallas as pl
from jax.experimental.pallas import tpu as pltpu
from jax.sharding import PartitionSpec as P

norm_epsilon = 1e-06
momentum_decay = 0.9
step_size = 0.01
root_half = 0.7071067811865476
inv_root_tau = 0.3989422804014327
MESH = pl.DeviceIdType.MESH
bf16 = jnp.bfloat16
f32 = jnp.float32


def times_transpose(left, right):
    return lax.dot_general(
        left, right, (((1,), (1,)), ((), ())), preferred_element_type=f32
    )


def contract_rows(left, right):
    return lax.dot_general(
        left, right, (((0,), (0,)), ((), ())), preferred_element_type=f32
    )


def relay_kernel(
    sections, replicas, micro, rows, model, width, tile, ahead,
    inputs_hbm, top_hbm, up_hbm, down_hbm, moment_up_hbm, moment_down_hbm,
    new_up, new_down, new_moment_up, new_moment_down,
    w_up, w_down, x_buf, hidden, slope, normed, scale_buf, grad_pre, grad_low, e_buf, sent,
    part_up, part_down, ring_up, ring_down, pair_up, pair_down, swap_up, swap_down,
    far_up, far_down, moment_up, moment_down, low_up, low_down, their_up, their_down,
    held_up, held_down,
    w_sem, own_sem, swap_send, swap_recv, top_send, e_recv, e_send,
    state_sem, moment_send, moment_recv, ring_send, ring_recv, pair_send, pair_recv,
    give_send, give_recv,
):
    section = lax.axis_index("section")
    replica = lax.axis_index("dp")
    core = lax.rem(replica, 2)
    other = replica + 1 - 2 * core
    side = lax.rem(replica // 2, 2)
    layer = replica // 4
    layers = replicas // 4
    above = lax.rem(replica + 4, replicas)
    below = lax.rem(replica + replicas - 4, replicas)
    beside = replica + 2 - 4 * side
    mirror = sections - 1 - section
    position = jnp.where(core == 0, sections - 1 - section, section)
    step_to = 2 * core - 1
    after = lax.rem(section + step_to + sections, sections)
    before = lax.rem(section - step_to + sections, sections)
    chunks = 2 * micro
    last = sections - 1
    parts = (part_up, part_down)
    rings = (ring_up, ring_down)
    pairs = (pair_up, pair_down)
    swaps = (swap_up, swap_down)
    fars = (far_up, far_down)
    lows = (low_up, low_down)
    theirs = (their_up, their_down)
    moments = (moment_up, moment_down)
    helds = (held_up, held_down)
    halves = (model // (2 * layers), width // (2 * layers))

    w_up_copy = pltpu.make_async_copy(up_hbm.at[core, 0], w_up, w_sem.at[0])
    w_down_copy = pltpu.make_async_copy(down_hbm.at[core, 0], w_down, w_sem.at[1])

    def aligned(start, size):
        return pl.ds(pl.multiple_of(start, size), size)

    def own_copy(slot):
        return pltpu.make_async_copy(
            inputs_hbm.at[core, slot], x_buf.at[2 * slot + core], own_sem.at[slot]
        )

    def remote(src, dst, send, recv, device):
        return pltpu.make_async_remote_copy(
            src_ref=src, dst_ref=dst, send_sem=send, recv_sem=recv,
            device_id=device, device_id_type=MESH,
        )

    def swap_copy(slot):
        return remote(
            inputs_hbm.at[1 - core, slot], x_buf.at[2 * slot + core],
            swap_send.at[slot], swap_recv.at[slot], (section, other),
        )

    def top_own(slot):
        return pltpu.make_async_copy(
            top_hbm.at[core, slot], e_buf.at[2 * slot + core], e_recv.at[2 * slot + core]
        )

    def top_swap(slot):
        return remote(
            top_hbm.at[1 - core, slot], e_buf.at[2 * slot + core],
            top_send.at[slot], e_recv.at[2 * slot + core], (section, other),
        )

    def relay_copy(chunk):
        return remote(
            sent.at[chunk], e_buf.at[chunk], e_send.at[chunk], e_recv.at[chunk], (after, replica)
        )

    def moment_copy(kind):
        return remote(
            lows[kind], theirs[kind], moment_send.at[kind], moment_recv.at[kind], (mirror, replica)
        )

    def ring_block(way, step):
        shift = layers - 1 - step if way == 0 else 1 + step
        return lax.rem(layer + shift, layers)

    def ring_copy(kind, way, step):
        half = halves[kind]
        start = ring_block(way, step) * 2 * half + way * half
        return remote(
            parts[kind].at[aligned(start, half), :], rings[kind].at[way, step],
            ring_send.at[kind, way, step], ring_recv.at[kind, way, step],
            (section, above if way == 0 else below),
        )

    def pair_copy(kind):
        half = halves[kind]
        start = layer * 2 * half + (1 - side) * half
        return remote(
            parts[kind].at[aligned(start, half), :], pairs[kind],
            pair_send.at[kind], pair_recv.at[kind], (section, beside),
        )

    def final_rows(kind, which):
        half = halves[kind]
        quarter = half // 2
        return aligned(layer * 2 * half + side * half + which * quarter, quarter)

    def give_copies(kind):
        return (
            remote(
                parts[kind].at[final_rows(kind, core), :], fars[kind].at[0],
                give_send.at[kind, 0], give_recv.at[kind, 0], (mirror, replica),
            ),
            remote(
                parts[kind].at[final_rows(kind, 1 - core), :], fars[kind].at[1],
                give_send.at[kind, 1], give_recv.at[kind, 1], (mirror, other),
            ),
            remote(
                parts[kind].at[final_rows(kind, 1 - core), :], swaps[kind],
                give_send.at[kind, 2], give_recv.at[kind, 2], (section, other),
            ),
        )

    state_copies = []
    for kind, (held_hbm, moment_hbm) in enumerate(
        ((up_hbm, moment_up_hbm), (down_hbm, moment_down_hbm))
    ):
        state_copies.append(
            pltpu.make_async_copy(moment_hbm.at[0], moments[kind], state_sem.at[kind, 0])
        )
        count = helds[kind].shape[1]
        for c in range(2):
            state_copies.append(
                pltpu.make_async_copy(
                    held_hbm.at[c, 0, aligned(replica * count, count), :],
                    helds[kind].at[c], state_sem.at[kind, 1 + c],
                )
            )

    w_up_copy.start()
    for slot in range(micro):
        own_copy(slot).start()
    w_down_copy.start()
    for copy in state_copies:
        copy.start()

    barrier = pltpu.get_barrier_semaphore()
    for device in (
        (after, replica), (before, replica), (section, other), (section, above),
        (section, below), (section, beside), (mirror, replica), (mirror, other),
    ):
        pl.semaphore_signal(barrier, inc=1, device_id=device, device_id_type=MESH)
    pl.semaphore_wait(barrier, 8)

    @pl.when(position == last)
    def _():
        for slot in range(micro):
            top_swap(slot).start()

    for slot in range(micro):
        swap_copy(slot).start()

    @pl.when(position == 0)
    def _():
        for slot in range(micro):
            top_own(slot).start()

    w_up_copy.wait()
    for slot in range(micro):
        own_copy(slot).wait()
        swap_copy(slot).wait()
    w_down_copy.wait()

    def forward(chunk):
        x = x_buf[chunk]

        for n in range(width // tile):
            cols = pl.ds(n * tile, tile)
            preact = jnp.dot(x, w_up[:, cols], preferred_element_type=f32)
            cdf = 0.5 * (1.0 + lax.erf(preact * root_half))
            hidden[chunk, :, cols] = (preact * cdf).astype(bf16)
            grown = cdf + preact * jnp.exp(-0.5 * preact * preact) * inv_root_tau
            slope[chunk, :, cols] = grown.astype(bf16)
        summed = x.astype(f32) + jnp.dot(hidden[chunk], w_down[...], preferred_element_type=f32)
        centre = summed - jnp.mean(summed, axis=-1, keepdims=True)
        scale_inv = lax.rsqrt(jnp.mean(centre * centre, axis=-1, keepdims=True) + norm_epsilon)
        normed[chunk] = centre * scale_inv
        scale_buf[chunk] = jnp.broadcast_to(scale_inv, (rows, 128))

    def backward(chunk):
        pltpu.make_async_copy(sent.at[chunk], e_buf.at[chunk], e_recv.at[chunk]).wait()
        upstream = e_buf[chunk].astype(f32)
        y = normed[chunk]
        scale_inv = scale_buf[chunk][:, :1]
        grad_sum = scale_inv * (
            upstream
            - jnp.mean(upstream, axis=-1, keepdims=True)
            - y * jnp.mean(upstream * y, axis=-1, keepdims=True)
        )
        low = grad_sum.astype(bf16)
        place = aligned(chunk * rows, rows)
        grad_low[place, :] = low
        for n in range(width // tile):
            cols = pl.ds(n * tile, tile)
            grad = times_transpose(low, w_down[cols, :]) * slope[chunk, :, cols].astype(f32)
            grad_pre[place, cols] = grad.astype(bf16)

        @pl.when(position < last)
        def _():
            sent[chunk] = (grad_sum + times_transpose(grad_pre[place, :], w_up[...])).astype(bf16)
            relay_copy(chunk).start()

    lead = jnp.minimum(chunks, ahead * position)

    @pl.loop(0, 2 * chunks)
    def _(step):
        @pl.when(step < chunks)
        def _():
            forward(step)

        back = step - lead

        @pl.when(jnp.logical_and(back >= 0, back < chunks))
        def _():
            backward(back)

        @pl.when(step == chunks - 1)
        def _():
            for copy in state_copies:
                copy.wait()
            for kind in range(2):
                lows[kind][...] = moments[kind][...].astype(bf16)
                moment_copy(kind).start()

    total = chunks * rows
    span = min(256, 2 * halves[0])

    def up_block(block):
        @pl.loop(0, 2 * halves[0] // span)
        def _(t):
            cols = aligned(block * 2 * halves[0] + t * span, span)
            left = x_buf[:, :, cols].reshape(total, span)
            part_up[cols, :] = contract_rows(left, grad_pre[...]).astype(bf16)

    def down_block(block):
        @pl.loop(0, 2 * halves[1] // span)
        def _(t):
            cols = aligned(block * 2 * halves[1] + t * span, span)
            left = hidden[:, :, cols].reshape(total, span)
            part_down[cols, :] = contract_rows(left, grad_low[...]).astype(bf16)

    def blocks(fill, shifts):
        @pl.loop(0, len(shifts))
        def _(i):
            shift = jnp.where(i == 0, shifts[0], shifts[-1])
            fill(lax.rem(layer + shift, layers))

    def first(kind, fill):
        fill(ring_block(0, 0))
        ring_copy(kind, 0, 0).start()
        fill(ring_block(1, 0))
        ring_copy(kind, 1, 0).start()

    def add_rows(kind, start, size, value):
        place = aligned(start, size)
        held = parts[kind][place, :].astype(f32) + value.astype(f32)
        parts[kind][place, :] = held.astype(bf16)

    def turn(kind, step):
        for way in range(2):
            ring_copy(kind, way, step).wait_recv()
            half = halves[kind]
            start = ring_block(way, step + 1) * 2 * half + way * half
            add_rows(kind, start, half, rings[kind][way, step])
            if step < layers - 2:
                ring_copy(kind, way, step + 1).start()

    def settle(kind):
        half = halves[kind]
        pair_copy(kind).start()
        pair_copy(kind).wait_recv()
        add_rows(kind, layer * 2 * half + side * half, half, pairs[kind][...])
        for copy in give_copies(kind):
            copy.start()

    rest = [2, 0]
    first(0, up_block)
    blocks(up_block, rest)
    first(1, down_block)
    turn(0, 0)
    blocks(down_block, rest)
    turn(1, 0)
    for step in range(1, layers - 2):
        turn(0, step)
        turn(1, step)
    turn(0, layers - 2)
    settle(0)
    turn(1, layers - 2)
    settle(1)

    for kind in range(2):
        moment_copy(kind).wait()

    for kind, (out, out_moment) in enumerate(
        ((new_up, new_moment_up), (new_down, new_moment_down))
    ):
        for copy in give_copies(kind):
            copy.wait_recv()
        own = parts[kind][final_rows(kind, core), :].astype(f32)
        got = swaps[kind][...].astype(f32)
        same = fars[kind][0].astype(f32)
        cross = fars[kind][1].astype(f32)
        zero = core == 0
        grad = jnp.where(zero, own + cross, got + same)
        grad_mirror = jnp.where(zero, got + same, own + cross)
        moment = momentum_decay * moments[kind][...] + grad
        out_moment[...] = moment
        out[0] = (helds[kind][0].astype(f32) - step_size * moment).astype(bf16)
        mirrored = momentum_decay * theirs[kind][...].astype(f32) + grad_mirror
        out[1] = (helds[kind][1].astype(f32) - step_size * mirrored).astype(bf16)

    for kind in range(2):
        for way in range(2):
            for step in range(layers - 1):
                ring_copy(kind, way, step).wait_send()
        pair_copy(kind).wait_send()
        for copy in give_copies(kind):
            copy.wait_send()

    @pl.when(position < last)
    def _():
        for chunk in range(chunks):
            relay_copy(chunk).wait_send()

    @pl.when(position == last)
    def _():
        for slot in range(micro):
            top_swap(slot).wait_send()


def relay(sections, replicas, ordered, top_grad, up_weight, down_weight, up_moment, down_moment):
    micro, rows, model = ordered.shape[1:]
    width = up_weight.shape[3]
    chunks = 2 * micro
    total = chunks * rows
    layers = replicas // 4
    half_up, half_down = model // (2 * layers), width // (2 * layers)
    held_up, held_down = half_up // 2, half_down // 2
    dma = pltpu.SemaphoreType.DMA
    flops = 2 * 6 * total * model * width
    return pl.pallas_call(
        functools.partial(
            relay_kernel, sections, replicas, micro, rows, model, width, min(512, width), 3
        ),
        out_shape=[
            jax.ShapeDtypeStruct((2, held_up, width), bf16),
            jax.ShapeDtypeStruct((2, held_down, model), bf16),
            jax.ShapeDtypeStruct((held_up, width), f32),
            jax.ShapeDtypeStruct((held_down, model), f32),
        ],
        in_specs=[pl.BlockSpec(memory_space=pl.ANY)] * 6,
        out_specs=[pl.BlockSpec(memory_space=pltpu.VMEM)] * 4,
        scratch_shapes=[
            pltpu.VMEM((model, width), bf16),
            pltpu.VMEM((width, model), bf16),
            pltpu.VMEM((chunks, rows, model), bf16),
            pltpu.VMEM((chunks, rows, width), bf16),
            pltpu.VMEM((chunks, rows, width), bf16),
            pltpu.VMEM((chunks, rows, model), f32),
            pltpu.VMEM((chunks, rows, 128), f32),
            pltpu.VMEM((total, width), bf16),
            pltpu.VMEM((total, model), bf16),
            pltpu.VMEM((chunks, rows, model), bf16),
            pltpu.VMEM((chunks, rows, model), bf16),
            pltpu.VMEM((model, width), bf16),
            pltpu.VMEM((width, model), bf16),
            pltpu.VMEM((2, layers - 1, half_up, width), bf16),
            pltpu.VMEM((2, layers - 1, half_down, model), bf16),
            pltpu.VMEM((half_up, width), bf16),
            pltpu.VMEM((half_down, model), bf16),
            pltpu.VMEM((held_up, width), bf16),
            pltpu.VMEM((held_down, model), bf16),
            pltpu.VMEM((2, held_up, width), bf16),
            pltpu.VMEM((2, held_down, model), bf16),
            pltpu.VMEM((held_up, width), f32),
            pltpu.VMEM((held_down, model), f32),
            pltpu.VMEM((held_up, width), bf16),
            pltpu.VMEM((held_down, model), bf16),
            pltpu.VMEM((held_up, width), bf16),
            pltpu.VMEM((held_down, model), bf16),
            pltpu.VMEM((2, held_up, width), bf16),
            pltpu.VMEM((2, held_down, model), bf16),
            dma((2,)),
            dma((micro,)),
            dma((micro,)),
            dma((micro,)),
            dma((micro,)),
            dma((chunks,)),
            dma((chunks,)),
            dma((2, 3)),
            dma((2,)),
            dma((2,)),
            dma((2, 2, layers - 1)),
            dma((2, 2, layers - 1)),
            dma((2,)),
            dma((2,)),
            dma((2, 3)),
            dma((2, 3)),
        ],
        compiler_params=pltpu.CompilerParams(
            collective_id=0, has_side_effects=True, vmem_limit_bytes=60 * 1024 * 1024
        ),
        cost_estimate=pl.CostEstimate(flops=flops, bytes_accessed=24 << 20, transcendentals=0),
    )(ordered, top_grad, up_weight, down_weight, up_moment, down_moment)


def on_device(section_inputs, top_grad, plan, up_weight, down_weight, up_moment, down_moment):
    ordered = jnp.stack([section_inputs[c, 0][plan[c]] for c in range(2)])
    new_up, new_down, moment_up, moment_down = relay(
        lax.axis_size("section"), lax.axis_size("dp"),
        ordered, top_grad, up_weight, down_weight, up_moment, down_moment,
    )
    return (new_up[:, None], new_down[:, None], moment_up[None], moment_down[None])


def solution(mesh):
    in_specs = (
        P(None, "section", None, "dp", None),
        P(None, None, "dp", None),
        P(),
        P(None, "section", None, None),
        P(None, "section", None, None),
        P("section", "dp", None),
        P("section", "dp", None),
    )
    out_specs = (
        P(None, "section", "dp", None),
        P(None, "section", "dp", None),
        P("section", "dp", None),
        P("section", "dp", None),
    )
    return jax.shard_map(
        on_device, mesh=mesh, in_specs=in_specs, out_specs=out_specs, check_vma=False
    )
```

time: 367 us -> 196 us (0.53)
  the two profiles are of different devices: /device:TPU:31 before, /device:TPU:24 now
where the time goes in v2:
time: 196 us
  Pallas kernels  184 us (94%)
  local copies, waits for them, and re-layouts  8.48 us (4%)
  other arithmetic  2.29 us (1%)
    pallas_call x1, Pallas kernels, relay(): pl.pallas_call(functools.partial(relay_kernel, sections, replicas, micro,...  184 us
    unnamed x8, local copies, waits for them, and re-layouts  5.43 us

profile of v2, /device:TPU:24, one launch (start us, length us, event | category | flops | bytes accessed | tf_op | source)
XLA Modules:
  0.0 195.8 jit_solution(6967256531312632027)
XLA Ops:
  0.6 0.8 fusion
  1.4 1.8 slice_bitcast_fusion.1
  3.2 0.6 gather_fusion
  3.9 0.6 gather_fusion.1
  4.5 1.5 pad_maximum_fusion.inputs_hbm
  6.0 184.3 %shard_map.102 = (bf16[2,64,2048]{2,1,0:T(8,128)(2,1)}, bf16[2,128,1024]{2,1,0:T(8,128)(2,1)}, f32[64,2048]{1,0:T(8,128)}, f32[128,1024]{1,0:T(8,128)}) custom-call(bf16[2,4,128,1024]{3,2,1,0:T(8,128)(2,1)} %pad_maximum_fusion.inputs_hbm, bf16[2,4,128,1024]{3,2,1,0:T(8,128)(2,1)} %top_hbm.1, bf16[2,1,1024,2048]{3,2,1,0:T(8,128)(2,1)} %up_hbm.1, ...), custom_call_target="tpu_custom_call" | custom-call | flops 25769803776 | bytes 25165824 | tf_op jit(solution)/shard_map/pallas_call | solution.py:385
  190.3 0.0 copy-start.1
  190.3 0.0 copy-start
  190.3 2.0 %copy.17 = bf16[2,1,64,2048]{3,2,1,0:T(8,128)(2,1)} copy(bf16[2,1,64,2048]{3,2,1,0:T(8,128)(2,1)} %bitcast.27) | data formatting | bytes 1048576
  192.3 1.9 copy.18
  194.2 0.0 copy-done.1
  194.2 0.8 copy.19
  195.0 0.0 copy-done
  195.0 0.8 copy.20
  (1 shorter events, 0.0 us)
Async XLA Ops:
  190.3 3.9 %copy-start.1 = (f32[64,2048]{1,0:T(8,128)S(1)}, f32[64,2048]{1,0:T(8,128)}, u32[]{:S(2)}) copy-start(f32[64,2048]{1,0:T(8,128)} %get-tuple-element.10) | copy-start | bytes 1572868
  190.3 4.6 %copy-start = (f32[128,1024]{1,0:T(8,128)S(1)}, f32[128,1024]{1,0:T(8,128)}, u32[]{:S(2)}) copy-start(f32[128,1024]{1,0:T(8,128)} %get-tuple-element.11) | copy-start | bytes 1572868

commit v3 on v2

--- a/solution.py
+++ b/solution.py
@@ -17,12 +17,6 @@
 f32 = jnp.float32
 
 
-def times_transpose(left, right):
-    return lax.dot_general(
-        left, right, (((1,), (1,)), ((), ())), preferred_element_type=f32
-    )
-
-
 def contract_rows(left, right):
     return lax.dot_general(
         left, right, (((0,), (0,)), ((), ())), preferred_element_type=f32
@@ -31,9 +25,9 @@
 
 def relay_kernel(
     sections, replicas, micro, rows, model, width, tile, ahead,
-    inputs_hbm, top_hbm, up_hbm, down_hbm, moment_up_hbm, moment_down_hbm,
+    plan_ref, inputs_hbm, top_hbm, up_hbm, down_hbm, moment_up_hbm, moment_down_hbm,
     new_up, new_down, new_moment_up, new_moment_down,
-    w_up, w_down, x_buf, hidden, slope, normed, scale_buf, grad_pre, grad_low, e_buf, sent,
+    w_up, w_down, x_buf, x_plan, hidden, slope, normed, scale_buf, grad_pre, grad_low, e_buf, sent,
     part_up, part_down, ring_up, ring_down, pair_up, pair_down, swap_up, swap_down,
     far_up, far_down, moment_up, moment_down, low_up, low_down, their_up, their_down,
     held_up, held_down,
@@ -77,7 +71,7 @@
 
     def own_copy(slot):
         return pltpu.make_async_copy(
-            inputs_hbm.at[core, slot], x_buf.at[2 * slot + core], own_sem.at[slot]
+            inputs_hbm.at[core, 0, slot], x_buf.at[2 * slot + core], own_sem.at[slot]
         )
 
     def remote(src, dst, send, recv, device):
@@ -88,7 +82,7 @@
 
     def swap_copy(slot):
         return remote(
-            inputs_hbm.at[1 - core, slot], x_buf.at[2 * slot + core],
+            inputs_hbm.at[1 - core, 0, slot], x_buf.at[2 * slot + core],
             swap_send.at[slot], swap_recv.at[slot], (section, other),
         )
 
@@ -199,14 +193,30 @@
         for slot in range(micro):
             top_own(slot).start()
 
+    turned_down, turned_up = part_up, part_down
+    across = min(256, model)
+
     w_up_copy.wait()
+
+    @pl.loop(0, width // across)
+    def _(t):
+        cols = aligned(t * across, across)
+        turned_up[cols, :] = w_up[:, cols].T
+
+    w_down_copy.wait()
+
+    @pl.loop(0, width // across)
+    def _(t):
+        cols = aligned(t * across, across)
+        turned_down[:, cols] = w_down[cols, :].T
+
     for slot in range(micro):
         own_copy(slot).wait()
         swap_copy(slot).wait()
-    w_down_copy.wait()
 
     def forward(chunk):
-        x = x_buf[chunk]
+        x = x_buf[2 * plan_ref[core, chunk // 2] + lax.rem(chunk, 2)]
+        x_plan[chunk] = x
 
         for n in range(width // tile):
             cols = pl.ds(n * tile, tile)
@@ -236,12 +246,14 @@
         grad_low[place, :] = low
         for n in range(width // tile):
             cols = pl.ds(n * tile, tile)
-            grad = times_transpose(low, w_down[cols, :]) * slope[chunk, :, cols].astype(f32)
+            grad = jnp.dot(low, turned_down[:, cols], preferred_element_type=f32)
+            grad = grad * slope[chunk, :, cols].astype(f32)
             grad_pre[place, cols] = grad.astype(bf16)
 
         @pl.when(position < last)
         def _():
-            sent[chunk] = (grad_sum + times_transpose(grad_pre[place, :], w_up[...])).astype(bf16)
+            grad_in = jnp.dot(grad_pre[place, :], turned_up[...], preferred_element_type=f32)
+            sent[chunk] = (grad_sum + grad_in).astype(bf16)
             relay_copy(chunk).start()
 
     lead = jnp.minimum(chunks, ahead * position)
@@ -273,7 +285,7 @@
         @pl.loop(0, 2 * halves[0] // span)
         def _(t):
             cols = aligned(block * 2 * halves[0] + t * span, span)
-            left = x_buf[:, :, cols].reshape(total, span)
+            left = x_plan[:, :, cols].reshape(total, span)
             part_up[cols, :] = contract_rows(left, grad_pre[...]).astype(bf16)
 
     def down_block(block):
@@ -372,8 +384,8 @@
             top_swap(slot).wait_send()
 
 
-def relay(sections, replicas, ordered, top_grad, up_weight, down_weight, up_moment, down_moment):
-    micro, rows, model = ordered.shape[1:]
+def relay(sections, replicas, plan, inputs, top_grad, up_weight, down_weight, up_moment, down_moment):
+    micro, rows, model = inputs.shape[2:]
     width = up_weight.shape[3]
     chunks = 2 * micro
     total = chunks * rows
@@ -392,11 +404,12 @@
             jax.ShapeDtypeStruct((held_up, width), f32),
             jax.ShapeDtypeStruct((held_down, model), f32),
         ],
-        in_specs=[pl.BlockSpec(memory_space=pl.ANY)] * 6,
+        in_specs=[pl.BlockSpec(memory_space=pltpu.SMEM)] + [pl.BlockSpec(memory_space=pl.ANY)] * 6,
         out_specs=[pl.BlockSpec(memory_space=pltpu.VMEM)] * 4,
         scratch_shapes=[
             pltpu.VMEM((model, width), bf16),
             pltpu.VMEM((width, model), bf16),
+            pltpu.VMEM((chunks, rows, model), bf16),
             pltpu.VMEM((chunks, rows, model), bf16),
             pltpu.VMEM((chunks, rows, width), bf16),
             pltpu.VMEM((chunks, rows, width), bf16),
@@ -445,15 +458,30 @@
             collective_id=0, has_side_effects=True, vmem_limit_bytes=60 * 1024 * 1024
         ),
         cost_estimate=pl.CostEstimate(flops=flops, bytes_accessed=24 << 20, transcendentals=0),
-    )(ordered, top_grad, up_weight, down_weight, up_moment, down_moment)
+    )(plan, inputs, top_grad, up_weight, down_weight, up_moment, down_moment)
+
+
+def hand_on_kernel(*refs):
+    count = len(refs) // 2
+    for source, target in zip(refs[:count], refs[count:]):
+        target[...] = source[...]
+
+
+def hand_on(*values):
+    return pl.pallas_call(
+        hand_on_kernel,
+        out_shape=[jax.ShapeDtypeStruct(v.shape, v.dtype) for v in values],
+        in_specs=[pl.BlockSpec(memory_space=pltpu.VMEM)] * len(values),
+        out_specs=[pl.BlockSpec(memory_space=pltpu.VMEM)] * len(values),
+        compiler_params=pltpu.CompilerParams(vmem_limit_bytes=8 << 20),
+    )(*values)
 
 
 def on_device(section_inputs, top_grad, plan, up_weight, down_weight, up_moment, down_moment):
-    ordered = jnp.stack([section_inputs[c, 0][plan[c]] for c in range(2)])
-    new_up, new_down, moment_up, moment_down = relay(
-        lax.axis_size("section"), lax.axis_size("dp"),
-        ordered, top_grad, up_weight, down_weight, up_moment, down_moment,
-    )
+    new_up, new_down, moment_up, moment_down = hand_on(*relay(
+        lax.axis_size("section"), lax.axis_size("dp"), plan, section_inputs,
+        top_grad, up_weight, down_weight, up_moment, down_moment,
+    ))
     return (new_up[:, None], new_down[:, None], moment_up[None], moment_down[None])
 
 

time: 196 us -> 184 us (0.939)
  Pallas kernels: 184 us -> 179 us
  local copies, waits for them, and re-layouts: 8.48 us -> 4.16 us
  other arithmetic: 2.29 us -> 0 us
    pallas_call x1, Pallas kernels: 184 us -> 178 us  [relay(): pl.pallas_call(functools.partial(relay_kernel, sections, replicas, micro,...]
where the time goes in v3:
time: 184 us
  Pallas kernels  179 us (97%)
  local copies, waits for them, and re-layouts  4.16 us (2%)
    pallas_call x1, Pallas kernels, relay(): pl.pallas_call(functools.partial(relay_kernel, sections, replicas, micro,...  178 us
    unnamed x8, local copies, waits for them, and re-layouts  4.16 us

profile of v3, /device:TPU:24, one launch (start us, length us, event | category | flops | bytes accessed | tf_op | source)
XLA Modules:
  0.0 183.9 jit_solution(5282326132133612274)
XLA Ops:
  0.6 177.6 %shard_map.102 = (bf16[2,64,2048]{2,1,0:T(8,128)(2,1)}, bf16[2,128,1024]{2,1,0:T(8,128)(2,1)}, f32[64,2048]{1,0:T(8,128)}, f32[128,1024]{1,0:T(8,128)}) custom-call(s32[2,4]{1,0:T(2,128)} %plan_ref.1, bf16[2,1,4,128,1024]{4,3,2,1,0:T(8,128)(2,1)} %inputs_hbm.1, bf16[2,4,128,1024]{3,2,1,0:T(8,128)(2,1)} %top_hbm.1, bf16[2,1,1024,2048]{3,2,1,0:T(8,128)(2,1)} %up_hbm.1, ...), custom_call_target="tpu_custom_call" | custom-call | flops 25769803776 | bytes 25165824 | tf_op jit(solution)/shard_map/pallas_call | solution.py:397
  178.3 0.0 copy-start
  178.3 1.0 copy-done
  179.3 0.0 copy-start.1
  179.3 1.0 copy-done.1
  180.4 0.0 copy-start.2
  180.4 1.0 copy-done.2
  181.4 0.0 copy-start.3
  181.4 1.0 copy-done.3
  182.5 1.4 shard_map.103
Async XLA Ops:
  178.3 1.0 copy-start
  179.3 1.0 copy-start.1
  180.4 1.0 copy-start.2
  181.4 1.0 copy-start.3

commit v4 on v3

--- a/solution.py
+++ b/solution.py
@@ -28,7 +28,7 @@
     plan_ref, inputs_hbm, top_hbm, up_hbm, down_hbm, moment_up_hbm, moment_down_hbm,
     new_up, new_down, new_moment_up, new_moment_down,
     w_up, w_down, x_buf, x_plan, hidden, slope, normed, scale_buf, grad_pre, grad_low, e_buf, sent,
-    part_up, part_down, ring_up, ring_down, pair_up, pair_down, swap_up, swap_down,
+    part_up, part_down, ring_up, ring_c, ring_d, pair_up, pair_c, pair_d, swap_up, swap_down,
     far_up, far_down, moment_up, moment_down, low_up, low_down, their_up, their_down,
     held_up, held_down,
     w_sem, own_sem, swap_send, swap_recv, top_send, e_recv, e_send,
@@ -53,8 +53,13 @@
     chunks = 2 * micro
     last = sections - 1
     parts = (part_up, part_down)
-    rings = (ring_up, ring_down)
-    pairs = (pair_up, pair_down)
+    rings = (ring_up.at[0], ring_up.at[1], ring_c, ring_d)
+    pairs = (pair_up.at[0], pair_up.at[1], pair_c)
+    kinds = (0, 0, 1, 1)
+    spans = tuple(
+        pl.ds((piece % 2) * (size // 2), size // 2)
+        for piece, size in enumerate((width, width, model, model))
+    )
     swaps = (swap_up, swap_down)
     fars = (far_up, far_down)
     lows = (low_up, low_down)
@@ -111,21 +116,35 @@
         shift = layers - 1 - step if way == 0 else 1 + step
         return lax.rem(layer + shift, layers)
 
-    def ring_copy(kind, way, step):
-        half = halves[kind]
-        start = ring_block(way, step) * 2 * half + way * half
-        return remote(
-            parts[kind].at[aligned(start, half), :], rings[kind].at[way, step],
-            ring_send.at[kind, way, step], ring_recv.at[kind, way, step],
+    def ring_rows(piece, way, step):
+        half = halves[kinds[piece]]
+        start = ring_block(way, step) * 2 * half
+        if piece == 3:
+            return aligned(start + side * half + way * (half // 2), half // 2)
+        return aligned(start + way * half, half)
+
+    def ring_copy(piece, way, step):
+        return remote(
+            parts[kinds[piece]].at[ring_rows(piece, way, step), spans[piece]],
+            rings[piece].at[way, step],
+            ring_send.at[piece, way, step], ring_recv.at[piece, way, step],
             (section, above if way == 0 else below),
         )
 
-    def pair_copy(kind):
-        half = halves[kind]
+    def pair_copy(piece):
+        half = halves[kinds[piece]]
         start = layer * 2 * half + (1 - side) * half
         return remote(
-            parts[kind].at[aligned(start, half), :], pairs[kind],
-            pair_send.at[kind], pair_recv.at[kind], (section, beside),
+            parts[kinds[piece]].at[aligned(start, half), spans[piece]], pairs[piece],
+            pair_send.at[piece], pair_recv.at[piece], (section, beside),
+        )
+
+    def early_copy(block):
+        half = halves[1]
+        start = block * 2 * half + (1 - side) * half
+        return remote(
+            part_down.at[aligned(start, half), spans[3]], pair_d.at[block],
+            pair_send.at[3 + block], pair_recv.at[3 + block], (section, beside),
         )
 
     def final_rows(kind, which):
@@ -133,19 +152,21 @@
         quarter = half // 2
         return aligned(layer * 2 * half + side * half + which * quarter, quarter)
 
-    def give_copies(kind):
+    def give_copies(piece):
+        kind = kinds[piece]
+        cols = spans[piece]
         return (
             remote(
-                parts[kind].at[final_rows(kind, core), :], fars[kind].at[0],
-                give_send.at[kind, 0], give_recv.at[kind, 0], (mirror, replica),
+                parts[kind].at[final_rows(kind, core), cols], fars[kind].at[0, :, cols],
+                give_send.at[piece, 0], give_recv.at[piece, 0], (mirror, replica),
             ),
             remote(
-                parts[kind].at[final_rows(kind, 1 - core), :], fars[kind].at[1],
-                give_send.at[kind, 1], give_recv.at[kind, 1], (mirror, other),
+                parts[kind].at[final_rows(kind, 1 - core), cols], fars[kind].at[1, :, cols],
+                give_send.at[piece, 1], give_recv.at[piece, 1], (mirror, other),
             ),
             remote(
-                parts[kind].at[final_rows(kind, 1 - core), :], swaps[kind],
-                give_send.at[kind, 2], give_recv.at[kind, 2], (section, other),
+                parts[kind].at[final_rows(kind, 1 - core), cols], swaps[kind].at[:, cols],
+                give_send.at[piece, 2], give_recv.at[piece, 2], (section, other),
             ),
         )
 
@@ -279,79 +300,44 @@
                 moment_copy(kind).start()
 
     total = chunks * rows
-    span = min(256, 2 * halves[0])
+    up_rows, down_rows = 2 * halves[0], halves[1]
 
     def up_block(block):
-        @pl.loop(0, 2 * halves[0] // span)
-        def _(t):
-            cols = aligned(block * 2 * halves[0] + t * span, span)
-            left = x_plan[:, :, cols].reshape(total, span)
-            part_up[cols, :] = contract_rows(left, grad_pre[...]).astype(bf16)
-
-    def down_block(block):
-        @pl.loop(0, 2 * halves[1] // span)
-        def _(t):
-            cols = aligned(block * 2 * halves[1] + t * span, span)
-            left = hidden[:, :, cols].reshape(total, span)
-            part_down[cols, :] = contract_rows(left, grad_low[...]).astype(bf16)
-
-    def blocks(fill, shifts):
-        @pl.loop(0, len(shifts))
-        def _(i):
-            shift = jnp.where(i == 0, shifts[0], shifts[-1])
-            fill(lax.rem(layer + shift, layers))
-
-    def first(kind, fill):
-        fill(ring_block(0, 0))
-        ring_copy(kind, 0, 0).start()
-        fill(ring_block(1, 0))
-        ring_copy(kind, 1, 0).start()
-
-    def add_rows(kind, start, size, value):
-        place = aligned(start, size)
-        held = parts[kind][place, :].astype(f32) + value.astype(f32)
-        parts[kind][place, :] = held.astype(bf16)
-
-    def turn(kind, step):
+        cols = aligned(block * up_rows, up_rows)
+        left = x_plan[:, :, cols].reshape(total, up_rows)
+        part_up[cols, :] = contract_rows(left, grad_pre[...]).astype(bf16)
+
+    def down_block(block, which):
+        cols = aligned(block * 2 * down_rows + which * down_rows, down_rows)
+        left = hidden[:, :, cols].reshape(total, down_rows)
+        part_down[cols, :] = contract_rows(left, grad_low[...]).astype(bf16)
+
+    def add_rows(piece, place, value):
+        part = parts[kinds[piece]]
+        cols = spans[piece]
+        part[place, cols] = (part[place, cols].astype(f32) + value.astype(f32)).astype(bf16)
+
+    def turn(piece, step):
         for way in range(2):
-            ring_copy(kind, way, step).wait_recv()
-            half = halves[kind]
-            start = ring_block(way, step + 1) * 2 * half + way * half
-            add_rows(kind, start, half, rings[kind][way, step])
+            ring_copy(piece, way, step).wait_recv()
+            add_rows(piece, ring_rows(piece, way, step + 1), rings[piece][way, step])
             if step < layers - 2:
-                ring_copy(kind, way, step + 1).start()
-
-    def settle(kind):
-        half = halves[kind]
-        pair_copy(kind).start()
-        pair_copy(kind).wait_recv()
-        add_rows(kind, layer * 2 * half + side * half, half, pairs[kind][...])
-        for copy in give_copies(kind):
+                ring_copy(piece, way, step + 1).start()
+
+    def give(piece):
+        for copy in give_copies(piece):
             copy.start()
 
-    rest = [2, 0]
-    first(0, up_block)
-    blocks(up_block, rest)
-    first(1, down_block)
-    turn(0, 0)
-    blocks(down_block, rest)
-    turn(1, 0)
-    for step in range(1, layers - 2):
-        turn(0, step)
-        turn(1, step)
-    turn(0, layers - 2)
-    settle(0)
-    turn(1, layers - 2)
-    settle(1)
-
-    for kind in range(2):
-        moment_copy(kind).wait()
-
-    for kind, (out, out_moment) in enumerate(
-        ((new_up, new_moment_up), (new_down, new_moment_down))
-    ):
-        for copy in give_copies(kind):
-            copy.wait_recv()
+    def settle(piece):
+        half = halves[kinds[piece]]
+        pair_copy(piece).wait_recv()
+        add_rows(piece, aligned(layer * 2 * half + side * half, half), pairs[piece][...])
+        give(piece)
+
+    def update(kind, out, out_moment):
+        for piece in (2 * kind, 2 * kind + 1):
+            for copy in give_copies(piece):
+                copy.wait_recv()
         own = parts[kind][final_rows(kind, core), :].astype(f32)
         got = swaps[kind][...].astype(f32)
         same = fars[kind][0].astype(f32)
@@ -365,13 +351,86 @@
         mirrored = momentum_decay * theirs[kind][...].astype(f32) + grad_mirror
         out[1] = (helds[kind][1].astype(f32) - step_size * mirrored).astype(bf16)
 
+    order = (layers - 1, 1, 2, 0)
+
+    @pl.loop(0, 2)
+    def _(i):
+        up_block(lax.rem(layer + jnp.where(i == 0, order[0], order[1]), layers))
+
+        @pl.when(i == 0)
+        def _():
+            ring_copy(0, 0, 0).start()
+            ring_copy(1, 0, 0).start()
+
+        @pl.when(i == 1)
+        def _():
+            ring_copy(0, 1, 0).start()
+            ring_copy(1, 1, 0).start()
+
+    @pl.loop(0, layers)
+    def _(i):
+        shift = jnp.where(i == 0, order[0], jnp.where(i == 1, order[1], 2 * (3 - i)))
+        block = lax.rem(layer + shift, layers)
+        down_block(block, 1 - side)
+        early_copy(block).start()
+
+    @pl.loop(0, 2)
+    def _(i):
+        up_block(lax.rem(layer + jnp.where(i == 0, order[2], order[3]), layers))
+
+    @pl.loop(0, 2)
+    def _(i):
+        down_block(lax.rem(layer + i, layers), side)
+
+    turn(0, 0)
+    turn(1, 0)
+
+    @pl.loop(2, layers)
+    def _(i):
+        down_block(lax.rem(layer + i, layers), side)
+
+    turn(0, 1)
+    turn(1, 1)
+    for way in range(2):
+        ring_copy(2, way, 0).start()
+    turn(0, 2)
+    pair_copy(0).start()
+    turn(1, 2)
+    pair_copy(1).start()
+
+    @pl.loop(0, layers)
+    def _(block):
+        early_copy(block).wait_recv()
+        add_rows(3, aligned(block * 2 * down_rows + side * down_rows, down_rows), pair_d[block])
+
+    for way in range(2):
+        ring_copy(3, way, 0).start()
+    settle(0)
+    turn(2, 0)
+    settle(1)
+    turn(3, 0)
+    turn(2, 1)
+    turn(3, 1)
+    turn(2, 2)
+    pair_copy(2).start()
+    turn(3, 2)
+    give(3)
+    settle(2)
     for kind in range(2):
+        moment_copy(kind).wait()
+    update(0, new_up, new_moment_up)
+    update(1, new_down, new_moment_down)
+
+    for piece in range(4):
         for way in range(2):
             for step in range(layers - 1):
-                ring_copy(kind, way, step).wait_send()
-        pair_copy(kind).wait_send()
-        for copy in give_copies(kind):
+                ring_copy(piece, way, step).wait_send()
+        for copy in give_copies(piece):
             copy.wait_send()
+    for piece in range(3):
+        pair_copy(piece).wait_send()
+    for block in range(layers):
+        early_copy(block).wait_send()
 
     @pl.when(position < last)
     def _():
@@ -421,10 +480,12 @@
             pltpu.VMEM((chunks, rows, model), bf16),
             pltpu.VMEM((model, width), bf16),
             pltpu.VMEM((width, model), bf16),
-            pltpu.VMEM((2, layers - 1, half_up, width), bf16),
-            pltpu.VMEM((2, layers - 1, half_down, model), bf16),
-            pltpu.VMEM((half_up, width), bf16),
-            pltpu.VMEM((half_down, model), bf16),
+            pltpu.VMEM((2, 2, layers - 1, half_up, width // 2), bf16),
+            pltpu.VMEM((2, layers - 1, half_down, model // 2), bf16),
+            pltpu.VMEM((2, layers - 1, half_down // 2, model // 2), bf16),
+            pltpu.VMEM((2, half_up, width // 2), bf16),
+            pltpu.VMEM((half_down, model // 2), bf16),
+            pltpu.VMEM((layers, half_down, model // 2), bf16),
             pltpu.VMEM((held_up, width), bf16),
             pltpu.VMEM((held_down, model), bf16),
             pltpu.VMEM((2, held_up, width), bf16),
@@ -447,12 +508,12 @@
             dma((2, 3)),
             dma((2,)),
             dma((2,)),
-            dma((2, 2, layers - 1)),
-            dma((2, 2, layers - 1)),
-            dma((2,)),
-            dma((2,)),
-            dma((2, 3)),
-            dma((2, 3)),
+            dma((4, 2, layers - 1)),
+            dma((4, 2, layers - 1)),
+            dma((3 + layers,)),
+            dma((3 + layers,)),
+            dma((4, 3)),
+            dma((4, 3)),
         ],
         compiler_params=pltpu.CompilerParams(
             collective_id=0, has_side_effects=True, vmem_limit_bytes=60 * 1024 * 1024

time: 184 us -> 166 us (0.902)
  the two profiles are of different devices: /device:TPU:24 before, /device:TPU:31 now
where the time goes in v4:
time: 166 us
  Pallas kernels  161 us (97%)
  local copies, waits for them, and re-layouts  4.16 us (3%)
    pallas_call x1, Pallas kernels, relay(): pl.pallas_call(functools.partial(relay_kernel, sections, replicas, micro,...  160 us
    unnamed x8, local copies, waits for them, and re-layouts  4.16 us

profile of v4, /device:TPU:31, one launch (start us, length us, event | category | flops | bytes accessed | tf_op | source)
XLA Modules:
  0.0 166.0 jit_solution(776881473842060122)
XLA Ops:
  0.6 159.8 %shard_map.102 = (bf16[2,64,2048]{2,1,0:T(8,128)(2,1)}, bf16[2,128,1024]{2,1,0:T(8,128)(2,1)}, f32[64,2048]{1,0:T(8,128)}, f32[128,1024]{1,0:T(8,128)}) custom-call(s32[2,4]{1,0:T(2,128)} %plan_ref.1, bf16[2,1,4,128,1024]{4,3,2,1,0:T(8,128)(2,1)} %inputs_hbm.1, bf16[2,4,128,1024]{3,2,1,0:T(8,128)(2,1)} %top_hbm.1, bf16[2,1,1024,2048]{3,2,1,0:T(8,128)(2,1)} %up_hbm.1, ...), custom_call_target="tpu_custom_call" | custom-call | flops 25769803776 | bytes 25165824 | tf_op jit(solution)/shard_map/pallas_call | solution.py:456
  160.4 0.0 copy-start
  160.4 1.0 copy-done
  161.5 0.0 copy-start.1
  161.5 1.0 copy-done.1
  162.5 0.0 copy-start.2
  162.5 1.0 copy-done.2
  163.6 0.0 copy-start.3
  163.6 1.0 copy-done.3
  164.6 1.4 shard_map.103
Async XLA Ops:
  160.4 1.0 copy-start
  161.5 1.0 copy-start.1
  162.5 1.0 copy-start.2
  163.6 1.0 copy-start.3

commit v5 on v4

--- a/solution.py
+++ b/solution.py
@@ -190,8 +190,6 @@
     for slot in range(micro):
         own_copy(slot).start()
     w_down_copy.start()
-    for copy in state_copies:
-        copy.start()
 
     barrier = pltpu.get_barrier_semaphore()
     for device in (
@@ -234,6 +232,8 @@
     for slot in range(micro):
         own_copy(slot).wait()
         swap_copy(slot).wait()
+    for copy in state_copies:
+        copy.start()
 
     def forward(chunk):
         x = x_buf[2 * plan_ref[core, chunk // 2] + lax.rem(chunk, 2)]
@@ -367,32 +367,37 @@
             ring_copy(0, 1, 0).start()
             ring_copy(1, 1, 0).start()
 
-    @pl.loop(0, layers)
-    def _(i):
-        shift = jnp.where(i == 0, order[0], jnp.where(i == 1, order[1], 2 * (3 - i)))
-        block = lax.rem(layer + shift, layers)
-        down_block(block, 1 - side)
-        early_copy(block).start()
+    def place(shift):
+        return lax.rem(layer + shift, layers)
+
+    def down_early(shift):
+        down_block(place(shift), 1 - side)
+        early_copy(place(shift)).start()
 
     @pl.loop(0, 2)
     def _(i):
-        up_block(lax.rem(layer + jnp.where(i == 0, order[2], order[3]), layers))
+        down_early(jnp.where(i == 0, order[0], order[1]))
+
+    up_block(place(order[2]))
+    down_early(order[2])
+    turn(0, 0)
+    turn(1, 0)
+    down_early(order[3])
+    up_block(place(order[3]))
 
     @pl.loop(0, 2)
     def _(i):
-        down_block(lax.rem(layer + i, layers), side)
-
-    turn(0, 0)
-    turn(1, 0)
-
-    @pl.loop(2, layers)
-    def _(i):
-        down_block(lax.rem(layer + i, layers), side)
+        down_block(place(jnp.where(i == 0, order[0], order[1])), side)
 
     turn(0, 1)
     turn(1, 1)
     for way in range(2):
         ring_copy(2, way, 0).start()
+
+    @pl.loop(0, 2)
+    def _(i):
+        down_block(place(jnp.where(i == 0, order[2], order[3])), side)
+
     turn(0, 2)
     pair_copy(0).start()
     turn(1, 2)
@@ -522,19 +527,40 @@
     )(plan, inputs, top_grad, up_weight, down_weight, up_moment, down_moment)
 
 
-def hand_on_kernel(*refs):
-    count = len(refs) // 2
-    for source, target in zip(refs[:count], refs[count:]):
-        target[...] = source[...]
+def hand_on_kernel(count, *refs):
+    sources, targets = refs[:count], refs[count:2 * count]
+    staged, load_sem, store_sem = refs[2 * count:3 * count], refs[3 * count], refs[3 * count + 1]
+    loads = []
+    stores = []
+    for i in range(count):
+        half = sources[i].shape[0] // 2
+        for j in range(2):
+            rows = pl.ds(j * half, half)
+            loads.append(pltpu.make_async_copy(
+                sources[i].at[rows], staged[i].at[rows], load_sem.at[i, j]
+            ))
+            stores.append(pltpu.make_async_copy(
+                staged[i].at[rows], targets[i].at[rows], store_sem.at[i, j]
+            ))
+    for load in loads:
+        load.start()
+    for load, store in zip(loads, stores):
+        load.wait()
+        store.start()
+    for store in stores:
+        store.wait()
 
 
 def hand_on(*values):
+    count = len(values)
     return pl.pallas_call(
-        hand_on_kernel,
+        functools.partial(hand_on_kernel, count),
         out_shape=[jax.ShapeDtypeStruct(v.shape, v.dtype) for v in values],
-        in_specs=[pl.BlockSpec(memory_space=pltpu.VMEM)] * len(values),
-        out_specs=[pl.BlockSpec(memory_space=pltpu.VMEM)] * len(values),
-        compiler_params=pltpu.CompilerParams(vmem_limit_bytes=8 << 20),
+        in_specs=[pl.BlockSpec(memory_space=pl.ANY)] * count,
+        out_specs=[pl.BlockSpec(memory_space=pl.ANY)] * count,
+        scratch_shapes=[pltpu.VMEM(v.shape, v.dtype) for v in values]
+        + [pltpu.SemaphoreType.DMA((count, 2))] * 2,
+        compiler_params=pltpu.CompilerParams(vmem_limit_bytes=60 * 1024 * 1024),
     )(*values)
 
 

time: 166 us -> 162 us (0.976)
  local copies, waits for them, and re-layouts: 4.16 us -> 0 us
    unnamed x8 -> x0, local copies, waits for them, and re-layouts: 4.16 us -> none
where the time goes in v5:
time: 162 us; the launch traced here: 161 us
  Pallas kernels  161 us (99%)
    pallas_call x1, Pallas kernels, relay(): pl.pallas_call(functools.partial(relay_kernel, sections, replicas, micro,...  158 us

profile of v5, /device:TPU:31, one launch (start us, length us, event | category | flops | bytes accessed | tf_op | source)
XLA Modules:
  0.0 161.5 jit_solution(7122822871467326538)
XLA Ops:
  0.6 158.4 %shard_map.102 = (bf16[2,64,2048]{2,1,0:T(8,128)(2,1)}, bf16[2,128,1024]{2,1,0:T(8,128)(2,1)}, f32[64,2048]{1,0:T(8,128)}, f32[128,1024]{1,0:T(8,128)}) custom-call(s32[2,4]{1,0:T(2,128)} %plan_ref.1, bf16[2,1,4,128,1024]{4,3,2,1,0:T(8,128)(2,1)} %inputs_hbm.1, bf16[2,4,128,1024]{3,2,1,0:T(8,128)(2,1)} %top_hbm.1, bf16[2,1,1024,2048]{3,2,1,0:T(8,128)(2,1)} %up_hbm.1, ...), custom_call_target="tpu_custom_call" | custom-call | flops 25769803776 | bytes 25165824 | tf_op jit(solution)/shard_map/pallas_call | solution.py:461
  159.1 2.4 %shard_map.103 = (bf16[2,64,2048]{2,1,0:T(8,128)(2,1)}, bf16[2,128,1024]{2,1,0:T(8,128)(2,1)}, f32[64,2048]{1,0:T(8,128)}, f32[128,1024]{1,0:T(8,128)}) custom-call(bf16[2,64,2048]{2,1,0:T(8,128)(2,1)} %get-tuple-element.12.refs_0_, bf16[2,128,1024]{2,1,0:T(8,128)(2,1)} %get-tuple-element.13.refs_1_, f32[64,2048]{1,0:T(8,128)} %get-tuple-element.14.refs_2_, ...), custom_call_target="tpu_custom_call" | custom-call | tf_op jit(solution)/shard_map/pallas_call | solution.py:556

commit v6 on v5

--- a/solution.py
+++ b/solution.py
@@ -191,6 +191,9 @@
         own_copy(slot).start()
     w_down_copy.start()
 
+    for copy in state_copies:
+        copy.start()
+
     barrier = pltpu.get_barrier_semaphore()
     for device in (
         (after, replica), (before, replica), (section, other), (section, above),
@@ -215,6 +218,10 @@
     turned_down, turned_up = part_up, part_down
     across = min(256, model)
 
+    def send_moments():
+        for kind in range(2):
+            moment_copy(kind).start()
+
     w_up_copy.wait()
 
     @pl.loop(0, width // across)
@@ -229,11 +236,18 @@
         cols = aligned(t * across, across)
         turned_down[:, cols] = w_down[cols, :].T
 
+    for copy in state_copies:
+        copy.wait()
+    for kind in range(2):
+        lows[kind][...] = moments[kind][...].astype(bf16)
+
+    @pl.when(position > 0)
+    def _():
+        send_moments()
+
     for slot in range(micro):
         own_copy(slot).wait()
         swap_copy(slot).wait()
-    for copy in state_copies:
-        copy.start()
 
     def forward(chunk):
         x = x_buf[2 * plan_ref[core, chunk // 2] + lax.rem(chunk, 2)]
@@ -290,14 +304,6 @@
         @pl.when(jnp.logical_and(back >= 0, back < chunks))
         def _():
             backward(back)
-
-        @pl.when(step == chunks - 1)
-        def _():
-            for copy in state_copies:
-                copy.wait()
-            for kind in range(2):
-                lows[kind][...] = moments[kind][...].astype(bf16)
-                moment_copy(kind).start()
 
     total = chunks * rows
     up_rows, down_rows = 2 * halves[0], halves[1]
@@ -420,6 +426,11 @@
     pair_copy(2).start()
     turn(3, 2)
     give(3)
+
+    @pl.when(position == 0)
+    def _():
+        send_moments()
+
     settle(2)
     for kind in range(2):
         moment_copy(kind).wait()

time: 162 us -> 148 us (0.914)
  Pallas kernels: 161 us -> 148 us
    pallas_call x1, Pallas kernels: 158 us -> 145 us  [relay(): pl.pallas_call(functools.partial(relay_kernel, sections, replicas, micro,...]
where the time goes in v6:
time: 148 us
  Pallas kernels  148 us (100%)
    pallas_call x1, Pallas kernels, relay(): pl.pallas_call(functools.partial(relay_kernel, sections, replicas, micro,...  145 us

profile of v6, /device:TPU:31, one launch (start us, length us, event | category | flops | bytes accessed | tf_op | source)
XLA Modules:
  0.0 148.2 jit_solution(14169797832818805645)
XLA Ops:
  0.6 145.2 %shard_map.102 = (bf16[2,64,2048]{2,1,0:T(8,128)(2,1)}, bf16[2,128,1024]{2,1,0:T(8,128)(2,1)}, f32[64,2048]{1,0:T(8,128)}, f32[128,1024]{1,0:T(8,128)}) custom-call(s32[2,4]{1,0:T(2,128)} %plan_ref.1, bf16[2,1,4,128,1024]{4,3,2,1,0:T(8,128)(2,1)} %inputs_hbm.1, bf16[2,4,128,1024]{3,2,1,0:T(8,128)(2,1)} %top_hbm.1, bf16[2,1,1024,2048]{3,2,1,0:T(8,128)(2,1)} %up_hbm.1, ...), custom_call_target="tpu_custom_call" | custom-call | flops 25769803776 | bytes 25165824 | tf_op jit(solution)/shard_map/pallas_call | solution.py:472
  145.8 2.4 %shard_map.103 = (bf16[2,64,2048]{2,1,0:T(8,128)(2,1)}, bf16[2,128,1024]{2,1,0:T(8,128)(2,1)}, f32[64,2048]{1,0:T(8,128)}, f32[128,1024]{1,0:T(8,128)}) custom-call(bf16[2,64,2048]{2,1,0:T(8,128)(2,1)} %get-tuple-element.12.refs_0_, bf16[2,128,1024]{2,1,0:T(8,128)(2,1)} %get-tuple-element.13.refs_1_, f32[64,2048]{1,0:T(8,128)} %get-tuple-element.14.refs_2_, ...), custom_call_target="tpu_custom_call" | custom-call | tf_op jit(solution)/shard_map/pallas_call | solution.py:567

commit v7 on v6

--- a/solution.py
+++ b/solution.py
@@ -56,9 +56,10 @@
     rings = (ring_up.at[0], ring_up.at[1], ring_c, ring_d)
     pairs = (pair_up.at[0], pair_up.at[1], pair_c)
     kinds = (0, 0, 1, 1)
-    spans = tuple(
-        pl.ds((piece % 2) * (size // 2), size // 2)
-        for piece, size in enumerate((width, width, model, model))
+    cut = ring_c.shape[-1]
+    spans = (
+        pl.ds(0, width // 2), pl.ds(width // 2, width // 2),
+        pl.ds(0, cut), pl.ds(cut, model - cut),
     )
     swaps = (swap_up, swap_down)
     fars = (far_up, far_down)
@@ -191,8 +192,10 @@
         own_copy(slot).start()
     w_down_copy.start()
 
-    for copy in state_copies:
-        copy.start()
+    @pl.when(position > 0)
+    def _():
+        for copy in state_copies:
+            copy.start()
 
     barrier = pltpu.get_barrier_semaphore()
     for device in (
@@ -202,14 +205,14 @@
         pl.semaphore_signal(barrier, inc=1, device_id=device, device_id_type=MESH)
     pl.semaphore_wait(barrier, 8)
 
+    for slot in range(micro):
+        swap_copy(slot).start()
+
     @pl.when(position == last)
     def _():
         for slot in range(micro):
             top_swap(slot).start()
 
-    for slot in range(micro):
-        swap_copy(slot).start()
-
     @pl.when(position == 0)
     def _():
         for slot in range(micro):
@@ -219,7 +222,10 @@
     across = min(256, model)
 
     def send_moments():
+        for copy in state_copies:
+            copy.wait()
         for kind in range(2):
+            lows[kind][...] = moments[kind][...].astype(bf16)
             moment_copy(kind).start()
 
     w_up_copy.wait()
@@ -236,11 +242,6 @@
         cols = aligned(t * across, across)
         turned_down[:, cols] = w_down[cols, :].T
 
-    for copy in state_copies:
-        copy.wait()
-    for kind in range(2):
-        lows[kind][...] = moments[kind][...].astype(bf16)
-
     @pl.when(position > 0)
     def _():
         send_moments()
@@ -248,6 +249,11 @@
     for slot in range(micro):
         own_copy(slot).wait()
         swap_copy(slot).wait()
+
+    @pl.when(position == 0)
+    def _():
+        for copy in state_copies:
+            copy.start()
 
     def forward(chunk):
         x = x_buf[2 * plan_ref[core, chunk // 2] + lax.rem(chunk, 2)]
@@ -467,6 +473,7 @@
     layers = replicas // 4
     half_up, half_down = model // (2 * layers), width // (2 * layers)
     held_up, held_down = half_up // 2, half_down // 2
+    cut = model * 3 // 8
     dma = pltpu.SemaphoreType.DMA
     flops = 2 * 6 * total * model * width
     return pl.pallas_call(
@@ -497,11 +504,11 @@
             pltpu.VMEM((model, width), bf16),
             pltpu.VMEM((width, model), bf16),
             pltpu.VMEM((2, 2, layers - 1, half_up, width // 2), bf16),
-            pltpu.VMEM((2, layers - 1, half_down, model // 2), bf16),
-            pltpu.VMEM((2, layers - 1, half_down // 2, model // 2), bf16),
+            pltpu.VMEM((2, layers - 1, half_down, cut), bf16),
+            pltpu.VMEM((2, layers - 1, half_down // 2, model - cut), bf16),
             pltpu.VMEM((2, half_up, width // 2), bf16),
-            pltpu.VMEM((half_down, model // 2), bf16),
-            pltpu.VMEM((layers, half_down, model // 2), bf16),
+            pltpu.VMEM((half_down, cut), bf16),
+            pltpu.VMEM((layers, half_down, model - cut), bf16),
             pltpu.VMEM((held_up, width), bf16),
             pltpu.VMEM((held_down, model), bf16),
             pltpu.VMEM((2, held_up, width), bf16),

time: 148 us -> 146 us (0.986)
  Pallas kernels: 148 us -> 145 us
    pallas_call x1, Pallas kernels: 145 us -> 143 us  [relay(): pl.pallas_call(functools.partial(relay_kernel, sections, replicas, micro,...]
where the time goes in v7:
time: 146 us
  Pallas kernels  145 us (99%)
    pallas_call x1, Pallas kernels, relay(): pl.pallas_call(functools.partial(relay_kernel, sections, replicas, micro,...  143 us

profile of v7, /device:TPU:31, one launch (start us, length us, event | category | flops | bytes accessed | tf_op | source)
XLA Modules:
  0.0 145.9 jit_solution(6595964226154030372)
XLA Ops:
  0.6 142.8 %shard_map.102 = (bf16[2,64,2048]{2,1,0:T(8,128)(2,1)}, bf16[2,128,1024]{2,1,0:T(8,128)(2,1)}, f32[64,2048]{1,0:T(8,128)}, f32[128,1024]{1,0:T(8,128)}) custom-call(s32[2,4]{1,0:T(2,128)} %plan_ref.1, bf16[2,1,4,128,1024]{4,3,2,1,0:T(8,128)(2,1)} %inputs_hbm.1, bf16[2,4,128,1024]{3,2,1,0:T(8,128)(2,1)} %top_hbm.1, bf16[2,1,1024,2048]{3,2,1,0:T(8,128)(2,1)} %up_hbm.1, ...), custom_call_target="tpu_custom_call" | custom-call | flops 25769803776 | bytes 25165824 | tf_op jit(solution)/shard_map/pallas_call | solution.py:479
  143.5 2.4 %shard_map.103 = (bf16[2,64,2048]{2,1,0:T(8,128)(2,1)}, bf16[2,128,1024]{2,1,0:T(8,128)(2,1)}, f32[64,2048]{1,0:T(8,128)}, f32[128,1024]{1,0:T(8,128)}) custom-call(bf16[2,64,2048]{2,1,0:T(8,128)(2,1)} %get-tuple-element.12.refs_0_, bf16[2,128,1024]{2,1,0:T(8,128)(2,1)} %get-tuple-element.13.refs_1_, f32[64,2048]{1,0:T(8,128)} %get-tuple-element.14.refs_2_, ...), custom_call_target="tpu_custom_call" | custom-call | tf_op jit(solution)/shard_map/pallas_call | solution.py:574

commit v8 on v7

--- a/solution.py
+++ b/solution.py
@@ -422,10 +422,10 @@
 
     for way in range(2):
         ring_copy(3, way, 0).start()
+    turn(2, 0)
     settle(0)
-    turn(2, 0)
+    turn(3, 0)
     settle(1)
-    turn(3, 0)
     turn(2, 1)
     turn(3, 1)
     turn(2, 2)

time: 146 us -> 145 us (level)
  no operation moved by 1% of the time
where the time goes in v8:
time: 145 us
  Pallas kernels  144 us (99%)
    pallas_call x1, Pallas kernels, relay(): pl.pallas_call(functools.partial(relay_kernel, sections, replicas, micro,...  142 us

profile of v8, /device:TPU:31, one launch (start us, length us, event | category | flops | bytes accessed | tf_op | source)
XLA Modules:
  0.0 144.9 jit_solution(2630864341019788839)
XLA Ops:
  0.6 141.9 %shard_map.102 = (bf16[2,64,2048]{2,1,0:T(8,128)(2,1)}, bf16[2,128,1024]{2,1,0:T(8,128)(2,1)}, f32[64,2048]{1,0:T(8,128)}, f32[128,1024]{1,0:T(8,128)}) custom-call(s32[2,4]{1,0:T(2,128)} %plan_ref.1, bf16[2,1,4,128,1024]{4,3,2,1,0:T(8,128)(2,1)} %inputs_hbm.1, bf16[2,4,128,1024]{3,2,1,0:T(8,128)(2,1)} %top_hbm.1, bf16[2,1,1024,2048]{3,2,1,0:T(8,128)(2,1)} %up_hbm.1, ...), custom_call_target="tpu_custom_call" | custom-call | flops 25769803776 | bytes 25165824 | tf_op jit(solution)/shard_map/pallas_call | solution.py:479
  142.5 2.4 %shard_map.103 = (bf16[2,64,2048]{2,1,0:T(8,128)(2,1)}, bf16[2,128,1024]{2,1,0:T(8,128)(2,1)}, f32[64,2048]{1,0:T(8,128)}, f32[128,1024]{1,0:T(8,128)}) custom-call(bf16[2,64,2048]{2,1,0:T(8,128)(2,1)} %get-tuple-element.12.refs_0_, bf16[2,128,1024]{2,1,0:T(8,128)(2,1)} %get-tuple-element.13.refs_1_, f32[64,2048]{1,0:T(8,128)} %get-tuple-element.14.refs_2_, ...), custom_call_target="tpu_custom_call" | custom-call | tf_op jit(solution)/shard_map/pallas_call | solution.py:574
